TPU v7x, 128 devices: a whole 4x4x4 slice. The times are simulated.
128 devices in a mesh: row: 16 (over y, z), col: 8 (over x, core).
Axes of the slice: x: 4, y: 4, z: 4, core: 2. Of those that a mesh axis runs over, the one named last changes fastest.
Arguments:
- inputs: bfloat16 [768, 8192], P('row', 'col'), may hold values from -16 to 16
- norm_gain: float32 [8192], P('col'), may hold values from 0.25 to 4
- w_gate: bfloat16 [8192, 28672], P('col', 'row'), may hold values from -0.09375 to 0.09375
- w_up: bfloat16 [8192, 28672], P('col', 'row'), may hold values from -0.09375 to 0.09375
- w_down: bfloat16 [28672, 8192], P('row', 'col'), may hold values from -0.050111483 to 0.050111483
- mask_gate: int32 [128, 448], P('col', 'row'), may hold values 0 or 1
- mask_up: int32 [128, 448], P('col', 'row'), may hold values 0 or 1
- mask_down: int32 [448, 128], P('row', 'col'), may hold values 0 or 1
- grad_out: bfloat16 [768, 8192], P('row', 'col'), may hold values from -5 to 5
Outputs:
- output: bfloat16 [768, 8192], P('row', 'col')
- grad_inputs: bfloat16 [768, 8192], P('row', 'col')
- grad_gain: float32 [8192], P('col')
- grad_w_gate: bfloat16 [8192, 28672], P('col', 'row')
- grad_w_up: bfloat16 [8192, 28672], P('col', 'row')
- grad_w_down: bfloat16 [28672, 8192], P('row', 'col')
All inputs are finite; a program needn't handle non-finite values. No bound on the sum of `mask_gate` or of `mask_up` or of `mask_down` on one device may be relied on, other than what follows from the above.
Results may differ from a plain program's by a relative error of at most 0.02.
Values may be sent and summed in bfloat16 or wider, within the bound.
A program may use at most 128 MiB of HBM per device.

v0:
```python
import jax
import jax.numpy as jnp
from jax import lax
from jax.sharding import PartitionSpec as P

D = 8192
BLOCK = 64


epsilon = 1e-05


def expand_mask(weight, block_mask):
    mask_rows, mask_cols = block_mask.shape
    blocked = (
        weight.reshape(mask_rows, BLOCK, mask_cols, BLOCK)
        * block_mask.astype(jnp.bfloat16)[:, None, :, None]
    )
    return blocked.reshape(weight.shape)


def contract_rows(left, right):
    return lax.dot_general(
        left, right, (((0,), (0,)), ((), ())), preferred_element_type=jnp.float32
    )


def contract_cols(left, right):
    return lax.dot_general(
        left, right, (((1,), (1,)), ((), ())), preferred_element_type=jnp.float32
    )


def shards(inputs, norm_gain, w_gate, w_up, w_down, mask_gate, mask_up, mask_down, grad_out):
    gate_eff = expand_mask(w_gate, mask_gate)
    up_eff = expand_mask(w_up, mask_up)
    down_eff = expand_mask(w_down, mask_down)
    local_rows = inputs.shape[0]
    inputs_all, grads_all = (
        lax.all_gather(inputs, "row", axis=0, tiled=True),
        lax.all_gather(grad_out, "row", axis=0, tiled=True),
    )
    ff_width = w_gate.shape[1]
    inputs_wide = inputs_all.astype(jnp.float32)
    squares = lax.psum(jnp.sum(inputs_wide * inputs_wide, axis=1, keepdims=True), "col")
    inv_rms = lax.rsqrt(squares / D + epsilon)
    normed = inputs_wide * inv_rms
    hidden_in = (normed * norm_gain).astype(jnp.bfloat16)
    row_block = hidden_in
    projected = lax.psum_scatter(
        jnp.concatenate(
            [
                jnp.dot(row_block, gate_eff, preferred_element_type=jnp.float32),
                jnp.dot(row_block, up_eff, preferred_element_type=jnp.float32),
            ],
            axis=1,
        ).astype(jnp.bfloat16),
        "col",
        scatter_dimension=0,
        tiled=True,
    ).astype(jnp.float32)
    gate_value = projected[:, :ff_width]
    up_value = projected[:, ff_width:]
    sigmoid_gate = jax.nn.sigmoid(gate_value)
    silu_gate = gate_value * sigmoid_gate
    hidden = (silu_gate * up_value).astype(jnp.bfloat16)
    hidden_all = lax.all_gather(hidden, "col", axis=0, tiled=True)
    row_block = hidden_all
    mixed_out = lax.psum_scatter(
        jnp.dot(row_block, down_eff, preferred_element_type=jnp.float32).astype(jnp.bfloat16),
        "row",
        scatter_dimension=0,
        tiled=True,
    ).astype(jnp.float32)
    output = (inputs.astype(jnp.float32) + mixed_out).astype(jnp.bfloat16)
    grad_w_down = expand_mask(contract_rows(hidden_all, grads_all).astype(jnp.bfloat16), mask_down)
    row_block = grads_all
    d_hidden = lax.psum_scatter(
        contract_cols(row_block, down_eff).astype(jnp.bfloat16),
        "col",
        scatter_dimension=0,
        tiled=True,
    ).astype(jnp.float32)
    d_up = (d_hidden * silu_gate).astype(jnp.bfloat16)
    d_gate = (
        d_hidden * up_value * sigmoid_gate * (1.0 + gate_value * (1.0 - sigmoid_gate))
    ).astype(jnp.bfloat16)
    d_gate_all, d_up_all = (
        lax.all_gather(d_gate, "col", axis=0, tiled=True),
        lax.all_gather(d_up, "col", axis=0, tiled=True),
    )
    grad_w_gate = expand_mask(contract_rows(hidden_in, d_gate_all).astype(jnp.bfloat16), mask_gate)
    grad_w_up = expand_mask(contract_rows(hidden_in, d_up_all).astype(jnp.bfloat16), mask_up)
    d_norm_in = lax.psum_scatter(
        (contract_cols(d_gate_all, gate_eff) + contract_cols(d_up_all, up_eff)).astype(
            jnp.bfloat16
        ),
        "row",
        scatter_dimension=0,
        tiled=True,
    ).astype(jnp.float32)
    row_start = lax.axis_index("row") * local_rows
    normed_local = lax.dynamic_slice_in_dim(normed, row_start, local_rows, 0)
    inv_rms_local = lax.dynamic_slice_in_dim(inv_rms, row_start, local_rows, 0)
    gain_part = jnp.sum(d_norm_in * normed_local, axis=0)
    d_normed = d_norm_in * norm_gain
    inner_part = jnp.sum(d_normed * normed_local, axis=1, keepdims=True)
    row_inner = lax.psum(inner_part, "col") / D
    grad_gain = lax.psum(gain_part, "row")
    grad_inputs = (
        grad_out.astype(jnp.float32) + inv_rms_local * (d_normed - normed_local * row_inner)
    ).astype(jnp.bfloat16)
    return (output, grad_inputs, grad_gain, grad_w_gate, grad_w_up, grad_w_down)


def solution(mesh):
    in_specs = (
        P("row", "col"),
        P("col"),
        P("col", "row"),
        P("col", "row"),
        P("row", "col"),
        P("col", "row"),
        P("col", "row"),
        P("row", "col"),
        P("row", "col"),
    )
    out_specs = (
        P("row", "col"),
        P("row", "col"),
        P("col"),
        P("col", "row"),
        P("col", "row"),
        P("row", "col"),
    )
    return jax.shard_map(shards, mesh=mesh, in_specs=in_specs, out_specs=out_specs, check_vma=False)
```

profile of v0, /device:TPU:1, one launch (start us, length us, event | category | flops | bytes accessed | tf_op | source)
XLA Modules:
  0.0 429.9 jit_solution(8002237608971727164)
XLA Ops:
  7.2 0.0 all-gather.6.cloned.1.call-start
  7.2 0.7 all-gather.6.cloned.1.call-update
  7.9 0.0 all-gather.10.cloned.1.call-start
  7.9 0.7 all-gather.10.cloned.1.call-update
  8.6 0.0 reduce-scatter.5.cloned.1.call-start
  8.7 0.7 convert_element_type.77
  9.4 0.1 copy.19
  9.5 4.0 mul.142
  13.5 10.7 %mul.143 = bf16[1024,1792]{0,1:T(8,128)(2,1)} reshape(bf16[16,64,28,64]{1,0,3,2:T(8,128)(2,1)} %mul.142) | data formatting | bytes 7340032 | tf_op jit(solution)/shard_map/mul | solution.py:16
  24.2 5.9 %copy.20 = bf16[1024,1792]{0,1:T(8,128)(2,1)} copy(bf16[1024,1792]{1,0:T(8,128)(2,1)} %param.12) | data formatting | bytes 7340032 | tf_op args[3]
  30.1 0.1 copy.17
  30.2 4.0 mul.139
  34.2 10.7 %mul.140 = bf16[1024,1792]{0,1:T(8,128)(2,1)} reshape(bf16[16,64,28,64]{1,0,3,2:T(8,128)(2,1)} %mul.139) | data formatting | bytes 7340032 | tf_op jit(solution)/shard_map/mul | solution.py:16
  44.9 5.9 %copy.18 = bf16[1024,1792]{0,1:T(8,128)(2,1)} copy(bf16[1024,1792]{1,0:T(8,128)(2,1)} %param.11) | data formatting | bytes 7340032 | tf_op args[2]
  50.9 7.1 %mul.144 = bf16[1024,1792]{0,1:T(8,128)(2,1)} multiply(bf16[1024,1792]{0,1:T(8,128)(2,1)} %copy.20, bf16[1024,1792]{0,1:T(8,128)(2,1)} %mul.143) | non-fusion elementwise | flops 1835008 | bytes 11010048 | tf_op jit(solution)/shard_map/mul | solution.py:16
  57.9 3.7 mul.141
  61.6 1.8 fusion.3
  63.4 13.5 %psum.21 = f32[768,1]{0,1:T(1,128)S(1)} all-reduce(f32[768,1]{0,1:T(1,128)S(1)} %broadcast_in_dim.4), channel_id=1, replica_groups=mesh['row'=16,'col'=8] {'col'}, use_global_device_ids=true, to_apply=%region_1.0 | all-reduce | flops 768 | bytes 6144 | tf_op jit(solution)/shard_map/psum | solution.py:45
  77.0 5.8 %convolution_convert_fusion.4 = bf16[768,1792]{1,0:T(8,128)(2,1)S(1)} fusion(bf16[1024,1792]{0,1:T(8,128)(2,1)} %mul.144, f32[1024]{0:T(1024)S(1)} %copy-done.9, f32[768]{0:T(1024)S(1)} %get-tuple-element.8, bf16[768,1024]{1,0:T(8,128)(2,1)} %all-gather.6.cloned.1.call-done), kind=kOutput, calls=%fused_computation.7 | convolution fusion | flops 2823094272 | bytes 8002560 | tf_op jit(solution)/shard_map/dot_general | solution.py:54
  82.8 3.5 convolution_convert_fusion.5
  86.3 2.9 pad_maximum_fusion
  89.1 0.0 reduce-scatter.5.cloned.1.call-update
  89.2 0.0 reduce-scatter.9.cloned.1.call-start
  89.2 0.6 copy-done.11
  89.8 0.1 copy.21
  89.9 4.0 mul.147
  93.9 10.7 %mul.148 = bf16[1792,1024]{1,0:T(8,128)(2,1)} reshape(bf16[28,64,16,64]{3,2,1,0:T(8,128)(2,1)} %mul.147) | data formatting | bytes 7340032 | tf_op jit(solution)/shard_map/mul | solution.py:16
  104.6 8.1 %fusion.4 = bf16[768,1792]{1,0:T(8,128)(2,1)} fusion(bf16[768,1024]{1,0:T(8,128)(2,1)} %all-gather.10.cloned.1.call-done, bf16[1792,1024]{1,0:T(8,128)(2,1)} %param.13, bf16[1792,1024]{1,0:T(8,128)(2,1)} %mul.148), kind=kOutput, calls=%fused_computation.15 | convolution fusion | flops 2821783552 | bytes 11665408 | tf_op jit(solution)/shard_map/dot_general | solution.py:29
  112.8 0.0 reduce-scatter.9.cloned.1.call-update
  112.8 0.0 all-gather.12.cloned.1.call-start
  112.9 30.0 %reduce-scatter.5.cloned.1.call-done = bf16[96,3584]{1,0:T(8,128)(2,1)} async-done(((bf16[768,3584]{1,0:T(8,128)(2,1)}), bf16[96,3584]{1,0:T(8,128)(2,1)}) %reduce-scatter.5.cloned.1.call-update) | async-done | bytes 688144 | tf_op jit(solution)/shard_map/reduce_scatter | solution.py:50
  142.9 1.2 convert_element_type.78
  144.1 35.1 %reduce-scatter.9.cloned.1.call-done = bf16[96,1792]{1,0:T(8,128)(2,1)} async-done(((bf16[768,1792]{1,0:T(8,128)(2,1)}), bf16[96,1792]{1,0:T(8,128)(2,1)}) %reduce-scatter.9.cloned.1.call-update) | async-done | bytes 344080 | tf_op jit(solution)/shard_map/reduce_scatter | solution.py:78
  179.2 2.3 fusion.10
  181.5 0.0 all-gather.12.cloned.1.call-update
  181.5 0.0 all-gather.14.cloned.1.call-start
  181.6 0.5 all-gather.14.cloned.1.call-update
  182.1 0.0 all-gather.8.cloned.1.call-start
  182.2 0.7 all-gather.8.cloned.1.call-update
  182.9 0.0 reduce-scatter.11.cloned.1.call-start
  182.9 27.4 %all-gather.12.cloned.1.call-done = bf16[768,1792]{1,0:T(8,128)(2,1)} async-done(((bf16[96,1792]{1,0:T(8,128)(2,1)}), bf16[768,1792]{1,0:T(8,128)(2,1)}) %all-gather.12.cloned.1.call-update) | async-done | bytes 2752528 | tf_op jit(solution)/shard_map/all_gather | solution.py:89
  210.3 7.5 %fusion.20 = f32[768,1024]{1,0:T(8,128)} fusion(bf16[768,1792]{1,0:T(8,128)(2,1)} %all-gather.12.cloned.1.call-done, bf16[1024,1792]{0,1:T(8,128)(2,1)} %mul.141), kind=kOutput, calls=%fused_computation.42 | convolution fusion | flops 2818572288 | bytes 9568256 | tf_op jit(solution)/shard_map/dot_general | solution.py:29
  217.8 21.1 %all-gather.14.cloned.1.call-done = bf16[768,1792]{1,0:T(8,128)(2,1)} async-done(((bf16[96,1792]{1,0:T(8,128)(2,1)}), bf16[768,1792]{1,0:T(8,128)(2,1)}) %all-gather.14.cloned.1.call-update) | async-done | bytes 2752528 | tf_op jit(solution)/shard_map/all_gather | solution.py:90
  238.9 8.0 %add_convert_fusion = bf16[768,1024]{1,0:T(8,128)(2,1)} fusion(f32[768,1024]{1,0:T(8,128)} %fusion.20, bf16[768,1792]{1,0:T(8,128)(2,1)} %all-gather.14.cloned.1.call-done, bf16[1024,1792]{0,1:T(8,128)(2,1)} %mul.144), kind=kOutput, calls=%fused_computation.13 | convolution fusion | flops 2820145152 | bytes 11141120 | tf_op jit(solution)/shard_map/dot_general | solution.py:29
  246.9 0.0 reduce-scatter.11.cloned.1.call-update
  246.9 0.3 reduce-scatter.7.cloned.1.call-start
  247.1 20.5 %all-gather.8.cloned.1.call-done = bf16[768,1792]{1,0:T(8,128)(2,1)} async-done(((bf16[96,1792]{1,0:T(8,128)(2,1)}), bf16[768,1792]{1,0:T(8,128)(2,1)}) %all-gather.8.cloned.1.call-update) | async-done | bytes 2752528 | tf_op jit(solution)/shard_map/all_gather | solution.py:67
  267.6 8.2 %convolution_convert_fusion.6 = bf16[768,1024]{1,0:T(8,128)(2,1)} fusion(bf16[768,1792]{1,0:T(8,128)(2,1)} %all-gather.8.cloned.1.call-done, bf16[1792,1024]{1,0:T(8,128)(2,1)} %param.13, bf16[1792,1024]{1,0:T(8,128)(2,1)} %mul.148), kind=kOutput, calls=%fused_computation.16 | convolution fusion | flops 2821193728 | bytes 11665408 | tf_op jit(solution)/shard_map/dot_general | solution.py:70
  275.8 0.0 reduce-scatter.7.cloned.1.call-update
  275.8 5.9 %copy.24 = bf16[1024,1792]{1,0:T(8,128)(2,1)} copy(bf16[1024,1792]{0,1:T(8,128)(2,1)} %mul.143) | data formatting | bytes 7340032 | tf_op jit(solution)/shard_map/mul | solution.py:16
  281.7 5.9 %copy.23 = bf16[1024,1792]{1,0:T(8,128)(2,1)} copy(bf16[1024,1792]{0,1:T(8,128)(2,1)} %mul.140) | data formatting | bytes 7340032 | tf_op jit(solution)/shard_map/mul | solution.py:16
  287.6 0.1 dynamic-slice_bitcast_fusion
  287.7 1.9 convert_multiply_fusion
  289.6 1.2 copy-done.5
  290.8 7.5 %fusion.2 = bf16[1792,1024]{1,0:T(8,128)(2,1)} fusion(bf16[1792,1024]{1,0:T(8,128)(2,1)S(1)} %copy-done.5, bf16[768,1792]{1,0:T(8,128)(2,1)} %all-gather.8.cloned.1.call-done, bf16[768,1024]{1,0:T(8,128)(2,1)} %all-gather.10.cloned.1.call-done), kind=kOutput, calls=%fused_computation.11 | convolution fusion | flops 2822242304 | bytes 11665408 | tf_op jit(solution)/shard_map/dot_general | solution.py:23
  298.3 4.8 %fusion.1 = bf16[1024,1792]{1,0:T(8,128)(2,1)} fusion(bf16[1024,1792]{1,0:T(8,128)(2,1)S(1)} %copy-done.4, bf16[768,1792]{1,0:T(8,128)(2,1)S(1)} %copy-done.13, f32[1024]{0:T(1024)S(1)} %copy-done.9, f32[768]{0:T(1024)S(1)} %get-tuple-element.8, bf16[768,1024]{1,0:T(8,128)(2,1)S(1)} %copy-done.2), kind=kOutput, calls=%fused_computation.10 | convolution fusion | flops 2825388032 | bytes 11672576 | tf_op jit(solution)/shard_map/dot_general | solution.py:23
  303.1 4.8 %fusion = bf16[1024,1792]{1,0:T(8,128)(2,1)} fusion(bf16[1024,1792]{1,0:T(8,128)(2,1)S(1)} %copy-done.3, bf16[768,1792]{1,0:T(8,128)(2,1)S(1)} %copy-done.12, f32[1024]{0:T(1024)S(1)} %copy-done.9, f32[768]{0:T(1024)S(1)} %get-tuple-element.8, bf16[768,1024]{1,0:T(8,128)(2,1)S(1)} %copy-done.2), kind=kOutput, calls=%fused_computation.9 | convolution fusion | flops 2825388032 | bytes 11672576 | tf_op jit(solution)/shard_map/dot_general | solution.py:23
  308.0 35.6 %reduce-scatter.11.cloned.1.call-done = bf16[48,1024]{1,0:T(8,128)(2,1)} async-done(((bf16[768,1024]{1,0:T(8,128)(2,1)}), bf16[48,1024]{1,0:T(8,128)(2,1)}) %reduce-scatter.11.cloned.1.call-update) | async-done | bytes 98320 | tf_op jit(solution)/shard_map/reduce_scatter | solution.py:94
  343.6 1.1 fusion.18
  344.7 14.0 %psum.22 = f32[48,1]{0,1:T(1,128)S(1)} all-reduce(f32[48,1]{0,1:T(1,128)S(1)} %bitcast.29), channel_id=1, replica_groups=mesh['row'=16,'col'=8] {'col'}, use_global_device_ids=true, to_apply=%region_7.0 | all-reduce | flops 48 | bytes 384 | tf_op jit(solution)/shard_map/psum | solution.py:108
  358.7 31.7 %psum.23 = f32[1024]{0:T(1024)} all-reduce(f32[1024]{0:T(1024)S(1)} %get-tuple-element.6), channel_id=1, replica_groups=mesh['row'=16,'col'=8] {'row'}, use_global_device_ids=true, to_apply=%region_9.0 | all-reduce | flops 1024 | bytes 8192 | tf_op jit(solution)/shard_map/psum | solution.py:109
  390.5 29.6 %reduce-scatter.7.cloned.1.call-done = bf16[48,1024]{1,0:T(8,128)(2,1)} async-done(((bf16[768,1024]{1,0:T(8,128)(2,1)}), bf16[48,1024]{1,0:T(8,128)(2,1)}) %reduce-scatter.7.cloned.1.call-update) | async-done | bytes 98320 | tf_op jit(solution)/shard_map/reduce_scatter | solution.py:69
  420.1 1.6 add_convert_fusion.1
  421.7 1.7 fusion.17
  (33 shorter events, 0.1 us)
Async XLA Ops:
  7.2 54.5 %all-gather.6.cloned.1.call-start = ((), (), s32[]{:S(2)}) async-start(), calls=%async_computation.4 | async-start | bytes 1671168 | tf_op jit(solution)/shard_map/all_gather | solution.py:40
  7.9 96.7 %all-gather.10.cloned.1.call-start = ((), (), s32[]{:S(2)}) async-start(), calls=%async_computation.8 | async-start | bytes 1671168 | tf_op jit(solution)/shard_map/all_gather | solution.py:41
  8.6 134.2 %reduce-scatter.5.cloned.1.call-start = ((), (), s32[]{:S(2)}) async-start(), calls=%async_computation.5 | async-start | bytes 6193152 | tf_op jit(solution)/shard_map/reduce_scatter | solution.py:50
  24.2 6.0 %copy-start.10 = (s32[16,28]{1,0:T(8,128)S(1)}, s32[16,28]{1,0:T(8,128)}, u32[]{:S(2)}) copy-start(s32[16,28]{1,0:T(8,128)} %param.14) | copy-start | bytes 5380
  50.9 7.1 %copy-start = (bf16[1024,1792]{0,1:T(8,128)(2,1)S(1)}, bf16[1024,1792]{0,1:T(8,128)(2,1)}, u32[]{:S(2)}) copy-start(bf16[1024,1792]{0,1:T(8,128)(2,1)} %mul.140) | copy-start | bytes 11010052
  50.9 7.1 %copy-start.1 = (bf16[1024,1792]{0,1:T(8,128)(2,1)S(1)}, bf16[1024,1792]{0,1:T(8,128)(2,1)}, u32[]{:S(2)}) copy-start(bf16[1024,1792]{0,1:T(8,128)(2,1)} %copy.18) | copy-start | bytes 11010052
  57.9 19.0 %copy-start.9 = (f32[1024]{0:T(1024)S(1)}, f32[1024]{0:T(1024)}, u32[]{:S(2)}) copy-start(f32[1024]{0:T(1024)} %param.10) | copy-start | bytes 12292
  77.0 5.8 %copy-start.2 = (bf16[768,1024]{1,0:T(8,128)(2,1)S(1)}, bf16[768,1024]{1,0:T(8,128)(2,1)}, u32[]{:S(2)}) copy-start(bf16[768,1024]{1,0:T(8,128)(2,1)} %all-gather.6.cloned.1.call-done) | copy-start | bytes 4718596
  77.0 5.8 %copy-start.6 = (bf16[1024,1792]{0,1:T(8,128)(2,1)S(1)}, bf16[1024,1792]{0,1:T(8,128)(2,1)}, u32[]{:S(2)}) copy-start(bf16[1024,1792]{0,1:T(8,128)(2,1)} %mul.141) | copy-start | bytes 11010052
  89.1 0.7 copy-start.11
  89.2 90.1 %reduce-scatter.9.cloned.1.call-start = ((), (), s32[]{:S(2)}) async-start(), calls=%async_computation.9 | async-start | bytes 3096576 | tf_op jit(solution)/shard_map/reduce_scatter | solution.py:78
  112.8 97.5 %all-gather.12.cloned.1.call-start = ((), (), s32[]{:S(2)}) async-start(), calls=%async_computation.10 | async-start | bytes 3096576 | tf_op jit(solution)/shard_map/all_gather | solution.py:89
  181.5 57.3 %all-gather.14.cloned.1.call-start = ((), (), s32[]{:S(2)}) async-start(), calls=%async_computation.11 | async-start | bytes 3096576 | tf_op jit(solution)/shard_map/all_gather | solution.py:90
  182.1 85.5 %all-gather.8.cloned.1.call-start = ((), (), s32[]{:S(2)}) async-start(), calls=%async_computation.6 | async-start | bytes 3096576 | tf_op jit(solution)/shard_map/all_gather | solution.py:67
  182.9 160.7 %reduce-scatter.11.cloned.1.call-start = ((), (), s32[]{:S(2)}) async-start(), calls=%async_computation.12 | async-start | bytes 1671168 | tf_op jit(solution)/shard_map/reduce_scatter | solution.py:94
  246.9 173.2 %reduce-scatter.7.cloned.1.call-start = ((), (), s32[]{:S(2)}) async-start(), calls=%async_computation.7 | async-start | bytes 1671168 | tf_op jit(solution)/shard_map/reduce_scatter | solution.py:69
  287.6 3.2 copy-start.5
  290.8 7.5 %copy-start.4 = (bf16[1024,1792]{1,0:T(8,128)(2,1)S(1)}, bf16[1024,1792]{1,0:T(8,128)(2,1)}, u32[]{:S(2)}) copy-start(bf16[1024,1792]{1,0:T(8,128)(2,1)} %copy.24) | copy-start | bytes 11010052
  290.8 7.5 %copy-start.13 = (bf16[768,1792]{1,0:T(8,128)(2,1)S(1)}, bf16[768,1792]{1,0:T(8,128)(2,1)}, u32[]{:S(2)}) copy-start(bf16[768,1792]{1,0:T(8,128)(2,1)} %all-gather.14.cloned.1.call-done) | copy-start | bytes 8257540
  298.3 4.9 %copy-start.3 = (bf16[1024,1792]{1,0:T(8,128)(2,1)S(1)}, bf16[1024,1792]{1,0:T(8,128)(2,1)}, u32[]{:S(2)}) copy-start(bf16[1024,1792]{1,0:T(8,128)(2,1)} %copy.23) | copy-start | bytes 11010052
  298.3 4.9 %copy-start.12 = (bf16[768,1792]{1,0:T(8,128)(2,1)S(1)}, bf16[768,1792]{1,0:T(8,128)(2,1)}, u32[]{:S(2)}) copy-start(bf16[768,1792]{1,0:T(8,128)(2,1)} %all-gather.12.cloned.1.call-done) | copy-start | bytes 8257540
  303.1 117.0 %copy-start.7 = (bf16[48,1024]{1,0:T(8,128)(2,1)S(1)}, bf16[48,1024]{1,0:T(8,128)(2,1)}, u32[]{:S(2)}) copy-start(bf16[48,1024]{1,0:T(8,128)(2,1)} %param.9) | copy-start | bytes 294916
  303.1 118.5 %copy-start.8 = (bf16[48,1024]{1,0:T(8,128)(2,1)S(1)}, bf16[48,1024]{1,0:T(8,128)(2,1)}, u32[]{:S(2)}) copy-start(bf16[48,1024]{1,0:T(8,128)(2,1)} %param.17) | copy-start | bytes 294916
Sparse Core Ops, SparseCore 0:
  10.2 46.3 all-gather.5
  58.8 43.3 all-gather.9
  104.6 38.2 reduce-scatter.4
  145.2 34.0 reduce-scatter.8
  181.7 28.5 all-gather.11
  211.9 26.8 all-gather.13
  240.7 26.8 all-gather.7
  271.2 72.3 reduce-scatter.10
  347.1 72.9 reduce-scatter.6
where the time goes:
time: 432 us; the launch traced here: 430 us
  waiting for transfers between devices  202 us (47%)
  local copies, waits for them, and re-layouts  70 us (16%)
  blocking collectives  59.3 us (14%)
  matrix products  58.2 us (13%)
  other arithmetic  26 us (6%)
  between operations  14 us (3%)
    mul x8, local copies, waits for them, and re-layouts, expand_mask(): weight.reshape(mask_rows, BLOCK, mask_cols, BLOCK)  55.9 us
    reduce_scatter x1, waiting for transfers between devices, shards(): lax.psum_scatter((contract_cols(d_gate_all, gate_eff) + contract_cols(d_u...  35.6 us
    reduce_scatter x1, waiting for transfers between devices, shards(): lax.psum_scatter(contract_cols(row_block, down_eff).astype(jnp.bfloat16),...  35.1 us
    psum x1, blocking collectives, shards(): grad_gain = lax.psum(gain_part, 'row')  31.7 us
    reduce_scatter x1, waiting for transfers between devices, shards(): lax.psum_scatter(jnp.concatenate([jnp.dot(row_block, gate_eff, preferred_...  30 us
    reduce_scatter x1, waiting for transfers between devices, shards(): lax.psum_scatter(jnp.dot(row_block, down_eff, preferred_element_type=jnp....  29.6 us
    all_gather x1, waiting for transfers between devices, shards(): lax.all_gather(d_gate, 'col', axis=0, tiled=True)  27.4 us
    dot_general x3, matrix products, contract_cols(): lax.dot_general(left, right, (((1,), (1,)), ((), ())), preferred_element_...  23.6 us
  transfers between devices with their start and end apart: 9, of which 7 were waited for; matrix products, arithmetic and copies ran while one was open for 34% of the time, Pallas kernels for 0%

commit v1 on v0

v1 whole, which is shorter than its diff:
```python
import functools

import jax
import jax.numpy as jnp
from jax import lax
from jax.experimental import pallas as pl
from jax.experimental.pallas import tpu as pltpu
from jax.sharding import PartitionSpec as P

D = 8192
BLOCK = 64
EPSILON = 1e-05
MESH = pl.DeviceIdType.MESH
F32 = jnp.float32
BF16 = jnp.bfloat16

LOCAL = 48
CHUNKS = 3
SUB = 16
FEATS = 1024
UNITS = 1792
HALF = FEATS // 2
TILE = 256
COPIES = 320


def nt_dot(left, right):
    return lax.dot_general(left, right, (((1,), (1,)), ((), ())), preferred_element_type=F32)


def nn_dot(left, right):
    return lax.dot_general(left, right, (((1,), (0,)), ((), ())), preferred_element_type=F32)


def lane_fold(value):
    total = value[:, 0:128]
    for start in range(128, value.shape[1], 128):
        total = total + value[:, start : start + 128]
    return total


def layer(
    inputs, gain, w_gate, w_up, w_down, mask_gate, mask_up, mask_down, grad_out,
    output, grad_inputs, grad_gain, grad_w_gate, grad_w_up, grad_w_down,
    wg, wu, wd, eg, eu, ed, hid, cot, part, pair, fwd_a, fwd_b, from_l, from_r, act,
    row_part, row_in1, row_sum, row_in2, normed, inv_rms, d_norm,
    sq_own, sq_in, in_own, in_in, gn_own, gn_in, stage, turned,
    send_sem, recv_sem, load_sem, store_sem,
):
    row = lax.axis_index("row")
    col = lax.axis_index("col")
    y, z = row // 4, lax.rem(row, 4)
    x, core = col // 2, lax.rem(col, 2)

    def up(value, steps):
        return lax.rem(value + steps, 4)

    def at_x(steps, other=0):
        return (row, up(x, steps) * 2 + (1 - core if other else core))

    def at_y(steps):
        return (up(y, steps) * 4 + z, col)

    def at_z(steps):
        return (y * 4 + up(z, steps), col)

    partner = at_x(0, 1)
    started = []

    def send(src, dst, device):
        index = len(started)
        copy = pltpu.make_async_remote_copy(
            src_ref=src, dst_ref=dst, send_sem=send_sem.at[index], recv_sem=recv_sem.at[index],
            device_id=device, device_id_type=MESH,
        )
        copy.start()
        started.append(copy)
        return copy

    def arrive(copies):
        for copy in copies:
            copy.wait_recv()

    loads = [
        pltpu.make_async_copy(source, target, load_sem.at[index])
        for index, (source, target) in enumerate(((w_down, wd), (w_gate, wg), (w_up, wu)))
    ]
    for load in loads:
        load.start()

    barrier = pltpu.get_barrier_semaphore()
    neighbours = [partner]
    for steps in (1, 2, 3):
        neighbours += [at_x(steps), at_x(steps, 1), at_y(steps), at_z(steps)]
    for device in neighbours:
        pl.semaphore_signal(barrier, inc=1, device_id=device, device_id_type=MESH)

    for k in range(CHUNKS):
        cot[k, y, z] = grad_out[k * SUB : (k + 1) * SUB, :]
    wide = inputs[...].astype(F32)
    sq_own[...] = lane_fold(wide * wide)

    pl.semaphore_wait(barrier, len(neighbours))

    def all_col(own, into):
        copies = [send(own, into.at[0], partner)]
        for steps in (1, 2, 3):
            copies.append(send(own, into.at[2 * steps - 1], at_x(steps)))
            copies.append(send(own, into.at[2 * steps], at_x(steps, 1)))
        return copies

    def gather1(ref, k):
        copies = []
        for steps in (1, 2, 3):
            part_a = ref.at[k, y, z, :, pl.ds(0, HALF)]
            part_b = ref.at[k, y, z, :, pl.ds(HALF, HALF)]
            copies.append(send(part_a, part_a, at_z(steps)))
            copies.append(send(part_b, part_b, at_y(steps)))
        return copies

    def gather2(ref, k):
        copies = []
        for steps in (1, 2, 3):
            part_a = ref.at[k, y, :, :, pl.ds(0, HALF)]
            part_b = ref.at[k, :, z, :, pl.ds(HALF, HALF)]
            copies.append(send(part_a, part_a, at_y(steps)))
            copies.append(send(part_b, part_b, at_z(steps)))
        return copies

    squares = all_col(sq_own, sq_in)
    cot1 = [gather1(cot, k) for k in range(CHUNKS)]

    def widen(mask_ref, into):
        rows, blocks = mask_ref.shape
        width = blocks * BLOCK
        unit = lax.broadcasted_iota(jnp.int32, (blocks, width), 1)
        first = lax.broadcasted_iota(jnp.int32, (blocks, width), 0) * BLOCK
        spread = jnp.where((unit >= first) & (unit < first + BLOCK), 1.0, 0.0).astype(BF16)
        wide_mask = nn_dot(mask_ref[...].astype(F32).astype(BF16), spread)
        for r in range(rows):
            into[r] = jnp.broadcast_to(wide_mask[r : r + 1, :], (SUB, width)).astype(BF16)

    def mask_weights(ref, wide_mask, load):
        load.wait()

        def body(r, carry):
            kept = wide_mask[r]
            for piece in range(BLOCK // SUB):
                rows = pl.ds(pl.multiple_of(r * BLOCK + piece * SUB, SUB), SUB)
                ref[rows, :] = ref[rows, :] * kept
            return carry

        lax.fori_loop(0, wide_mask.shape[0], body, 0)

    widen(mask_down, ed)
    mask_weights(wd, ed, loads[0])

    arrive(squares)
    squares_all = sq_own[...]
    for index in range(7):
        squares_all = squares_all + sq_in[index]
    inv_rms[...] = jnp.broadcast_to(
        lax.rsqrt(jnp.sum(squares_all, axis=1, keepdims=True) / D + EPSILON), (LOCAL, 128)
    )
    scale = inv_rms[:, 0:1]
    normed[...] = inputs[...].astype(F32) * scale
    own_hidden_in = (normed[...] * gain[...]).astype(BF16)
    for k in range(CHUNKS):
        hid[k, y, z] = own_hidden_in[k * SUB : (k + 1) * SUB, :]
    hid1 = [gather1(hid, k) for k in range(CHUNKS)]

    arrive(cot1[0])
    cot2 = {0: gather2(cot, 0)}
    arrive(hid1[0])
    hid2 = {0: gather2(hid, 0)}
    for k in (1, 2):
        arrive(cot1[k])
        cot2[k] = gather2(cot, k)
        arrive(hid1[k])
        hid2[k] = gather2(hid, k)

    widen(mask_gate, eg)
    widen(mask_up, eu)
    mask_weights(wg, eg, loads[1])
    mask_weights(wu, eu, loads[2])

    def chunk_of(ref, k):
        return ref[k].reshape(CHUNKS and 4 * 4 * SUB, FEATS)

    def tiles(count, body):
        def step(n, carry):
            body(pl.multiple_of(n * TILE, TILE))
            return carry

        lax.fori_loop(0, count, step, 0)

    def pair_send(k, start, width):
        return [
            send(
                part.at[k, pl.ds(pl.multiple_of((1 - core) * 128, 128), 128), pl.ds(start, width)],
                pair.at[k, :, pl.ds(start, width)],
                partner,
            )
        ]

    def mm_down_back(k):
        arrive(cot2[k])

        def body(at):
            product = nt_dot(chunk_of(cot, k), wd[pl.ds(at, TILE), :])
            part[k, :, pl.ds(at, TILE)] = product.astype(BF16)

        tiles(UNITS // TILE, body)
        return pair_send(k, 0, UNITS)

    def mm_gate_up(k):
        arrive(hid2[k])

        def body(at):
            left = chunk_of(hid, k)
            part[k, :, pl.ds(UNITS + at, TILE)] = nn_dot(left, wg[:, pl.ds(at, TILE)]).astype(BF16)
            part[k, :, pl.ds(2 * UNITS + at, TILE)] = nn_dot(left, wu[:, pl.ds(at, TILE)]).astype(BF16)

        tiles(UNITS // TILE, body)
        return pair_send(k, UNITS, 2 * UNITS)

    def block_rows(which, offset, count):
        return pl.ds(pl.multiple_of(which * 32 + offset, SUB), count)

    def scatter1(k, job, copies):
        start, width = job
        cols = pl.ds(start, width)
        arrive(copies)
        mine = pl.multiple_of(core * 128, 128)
        def body(r, carry):
            rows = pl.ds(pl.multiple_of(r * SUB, SUB), SUB)
            own = part[k, pl.ds(pl.multiple_of(mine + r * SUB, SUB), SUB), cols].astype(F32)
            pair[k, rows, cols] = (own + pair[k, rows, cols].astype(F32)).astype(BF16)
            return carry
        lax.fori_loop(0, 8, body, 0)
        right, left = at_x(1), at_x(3)
        two = up(x, 2)
        return (
            send(pair.at[k, block_rows(two, 0, SUB), cols], fwd_a.at[k, :, cols], right),
            send(pair.at[k, block_rows(two, SUB, SUB), cols], fwd_b.at[k, :, cols], left),
            send(pair.at[k, block_rows(up(x, 1), SUB, SUB), cols], from_l.at[k, pl.ds(SUB, SUB), cols], right),
            send(pair.at[k, block_rows(up(x, 3), 0, SUB), cols], from_r.at[k, pl.ds(0, SUB), cols], left),
        )

    def scatter2(k, job, copies):
        start, width = job
        cols = pl.ds(start, width)
        right, left = at_x(1), at_x(3)
        arrive(copies[0:1])
        own = pair[k, block_rows(up(x, 1), 0, SUB), cols].astype(F32)
        fwd_a[k, :, cols] = (own + fwd_a[k, :, cols].astype(F32)).astype(BF16)
        first = send(fwd_a.at[k, :, cols], from_l.at[k, pl.ds(0, SUB), cols], right)
        arrive(copies[1:2])
        own = pair[k, block_rows(up(x, 3), SUB, SUB), cols].astype(F32)
        fwd_b[k, :, cols] = (own + fwd_b[k, :, cols].astype(F32)).astype(BF16)
        second = send(fwd_b.at[k, :, cols], from_r.at[k, pl.ds(SUB, SUB), cols], left)
        return (copies[2], copies[3], first, second)

    down_job, gate_up_job = (0, UNITS), (UNITS, 2 * UNITS)
    owner = core * 4 + x

    def activate(k, copies):
        arrive(copies)
        def total(start):
            cols = pl.ds(start, 256)
            return (
                pair[k, block_rows(x, 0, 32), cols].astype(F32)
                + from_l[k, :, cols].astype(F32)
                + from_r[k, :, cols].astype(F32)
            )

        def body(at):
            d_hidden = total(at)
            gate_value = total(UNITS + at)
            up_value = total(2 * UNITS + at)
            sigma = jax.nn.sigmoid(gate_value)
            silu = gate_value * sigma
            rows = block_rows(owner, 0, 32)
            act[k, rows, pl.ds(at, 256)] = (silu * up_value).astype(BF16)
            act[k, rows, pl.ds(UNITS + at, 256)] = (
                d_hidden * up_value * sigma * (1.0 + gate_value * (1.0 - sigma))
            ).astype(BF16)
            act[k, rows, pl.ds(2 * UNITS + at, 256)] = (d_hidden * silu).astype(BF16)

        tiles(UNITS // 256, body)
        block = act.at[k, block_rows(owner, 0, 32), :]
        return (
            send(block, block, at_x(1)),
            send(block, block, at_x(3)),
            send(block, block, partner),
        )

    def spread2(k, copies):
        from_left, from_right = core * 4 + up(x, 3), core * 4 + up(x, 1)
        arrive(copies[0:1])
        half = act.at[k, block_rows(from_left, 0, SUB), :]
        block = act.at[k, block_rows(from_left, 0, 32), :]
        first = send(half, half, at_x(1))
        first_pair = send(block, block, partner)
        arrive(copies[1:2])
        half = act.at[k, block_rows(from_right, SUB, SUB), :]
        block = act.at[k, block_rows(from_right, 0, 32), :]
        second = send(half, half, at_x(3))
        second_pair = send(block, block, partner)
        return (first, second), (copies[2], first_pair, second_pair)

    def spread3(k, halves, pairs):
        arrive(halves)
        block = act.at[k, block_rows(core * 4 + up(x, 2), 0, 32), :]
        return pairs + (send(block, block, partner),)

    def row_scatter1(which, k):
        copies = []
        for steps in (1, 2, 3):
            copies.append(send(
                row_part.at[which, k, up(y, steps), :, :, pl.ds(0, HALF)],
                row_in1.at[which, k, steps - 1, :, :, pl.ds(0, HALF)], at_y(steps)))
            copies.append(send(
                row_part.at[which, k, :, up(z, steps), :, pl.ds(HALF, HALF)],
                row_in1.at[which, k, steps - 1, :, :, pl.ds(HALF, HALF)], at_z(steps)))
        return copies

    def row_scatter2(which, k, copies):
        arrive(copies)
        sum_a = row_part[which, k, y, :, :, 0:HALF].astype(F32)
        sum_b = row_part[which, k, :, z, :, HALF:FEATS].astype(F32)
        for index in range(3):
            sum_a = sum_a + row_in1[which, k, index, :, :, 0:HALF].astype(F32)
            sum_b = sum_b + row_in1[which, k, index, :, :, HALF:FEATS].astype(F32)
        row_sum[which, k, :, :, 0:HALF] = sum_a.astype(BF16)
        row_sum[which, k, :, :, HALF:FEATS] = sum_b.astype(BF16)
        after = []
        for steps in (1, 2, 3):
            after.append(send(
                row_sum.at[which, k, up(z, steps), :, pl.ds(0, HALF)],
                row_in2.at[which, k, steps - 1, :, pl.ds(0, HALF)], at_z(steps)))
            after.append(send(
                row_sum.at[which, k, up(y, steps), :, pl.ds(HALF, HALF)],
                row_in2.at[which, k, steps - 1, :, pl.ds(HALF, HALF)], at_y(steps)))
        return after

    def row_total(which, k, copies, start):
        other = z if start == 0 else y
        total = row_sum[which, k, other, :, start : start + HALF].astype(F32)
        for index in range(3):
            total = total + row_in2[which, k, index, :, start : start + HALF].astype(F32)
        return total

    def mm_out(k, pairs):
        arrive(pairs)

        def body(at):
            product = nn_dot(act[k, :, 0:UNITS], wd[:, pl.ds(at, TILE)]).astype(BF16)
            row_part[0, k, :, :, :, pl.ds(at, TILE)] = product.reshape(4, 4, SUB, TILE)

        tiles(FEATS // TILE, body)
        return row_scatter1(0, k)

    def mm_in_back(k):
        def body(at):
            product = nt_dot(act[k, :, UNITS : 2 * UNITS], wg[pl.ds(at, TILE), :]) + nt_dot(
                act[k, :, 2 * UNITS : 3 * UNITS], wu[pl.ds(at, TILE), :]
            )
            row_part[1, k, :, :, :, pl.ds(at, TILE)] = product.astype(BF16).reshape(4, 4, SUB, TILE)

        tiles(FEATS // TILE, body)
        return row_scatter1(1, k)

    def finish_out(k, copies):
        arrive(copies)
        rows = slice(k * SUB, (k + 1) * SUB)
        for start in (0, HALF):
            total = row_total(0, k, copies, start)
            output[rows, start : start + HALF] = (
                inputs[rows, start : start + HALF].astype(F32) + total
            ).astype(BF16)

    def finish_in(k, copies):
        arrive(copies)
        rows = slice(k * SUB, (k + 1) * SUB)
        for start in (0, HALF):
            d_norm[rows, start : start + HALF] = row_total(1, k, copies, start)

    stores = []

    def weight_grad(left_of, right_of, units, width, wide_mask, target, slot):
        def rows_body(m, carry):
            at = pl.multiple_of(m * TILE, TILE)
            use = lax.rem(m, 2)
            turned[...] = left_of(at).T
            @pl.when(m >= 2)
            def _():
                pltpu.make_async_copy(
                    stage.at[use, :, pl.ds(0, width)], target.at[pl.ds(at, TILE), :], store_sem.at[slot + use]
                ).wait()

            def cols_body(n, inner):
                to = pl.multiple_of(n * TILE, TILE)
                product = nn_dot(turned[...], right_of(to)).astype(BF16)
                kept = wide_mask[pl.ds(m * 4, 4), :, pl.ds(to, TILE)]
                product = product.reshape(4, 4, SUB, TILE) * kept.reshape(4, 1, SUB, TILE)
                stage[use, :, pl.ds(to, TILE)] = product.reshape(TILE, TILE)
                return inner

            lax.fori_loop(0, width // TILE, cols_body, 0)
            pltpu.make_async_copy(
                stage.at[use, :, pl.ds(0, width)], target.at[pl.ds(at, TILE), :], store_sem.at[slot + use]
            ).start()
            return carry

        lax.fori_loop(0, units // TILE, rows_body, 0)
        for use in range(2):
            pltpu.make_async_copy(
                stage.at[use, :, pl.ds(0, width)], target.at[pl.ds(0, TILE), :], store_sem.at[slot + use]
            ).wait()

    tokens = CHUNKS * 256

    def act_cols(start):
        def get(at):
            return act[:, :, pl.ds(pl.multiple_of(start + at, TILE), TILE)].reshape(tokens, TILE)

        return get

    def token_cols(ref):
        def get(at):
            return ref[:, :, :, :, pl.ds(at, TILE)].reshape(tokens, TILE)

        return get

    pd0 = mm_down_back(0)
    pg0 = mm_gate_up(0)
    sd0 = scatter1(0, down_job, pd0)
    pd1 = mm_down_back(1)
    sg0 = scatter1(0, gate_up_job, pg0)
    td0 = scatter2(0, down_job, sd0)
    pg1 = mm_gate_up(1)
    sd1 = scatter1(1, down_job, pd1)
    tg0 = scatter2(0, gate_up_job, sg0)
    sg1 = scatter1(1, gate_up_job, pg1)
    td1 = scatter2(1, down_job, sd1)
    pd2 = mm_down_back(2)
    pg2 = mm_gate_up(2)
    a0 = activate(0, td0 + tg0)
    tg1 = scatter2(1, gate_up_job, sg1)
    sd2 = scatter1(2, down_job, pd2)
    h0, q0 = spread2(0, a0)
    sg2 = scatter1(2, gate_up_job, pg2)
    a1 = activate(1, td1 + tg1)
    td2 = scatter2(2, down_job, sd2)
    r0 = spread3(0, h0, q0)
    tg2 = scatter2(2, gate_up_job, sg2)
    h1, q1 = spread2(1, a1)
    o0 = mm_out(0, r0)
    n0 = mm_in_back(0)
    a2 = activate(2, td2 + tg2)
    r1 = spread3(1, h1, q1)
    h2, q2 = spread2(2, a2)
    o0 = row_scatter2(0, 0, o0)
    n0 = row_scatter2(1, 0, n0)
    o1 = mm_out(1, r1)
    n1 = mm_in_back(1)
    r2 = spread3(2, h2, q2)
    finish_out(0, o0)
    finish_in(0, n0)
    o1 = row_scatter2(0, 1, o1)
    n1 = row_scatter2(1, 1, n1)
    o2 = mm_out(2, r2)
    n2 = mm_in_back(2)
    weight_grad(act_cols(0), token_cols(cot), UNITS, FEATS, ed, grad_w_down, 0)
    o2 = row_scatter2(0, 2, o2)
    n2 = row_scatter2(1, 2, n2)
    finish_out(1, o1)
    finish_in(1, n1)
    weight_grad(token_cols(hid), act_cols(UNITS), FEATS, UNITS, eg, grad_w_gate, 0)
    finish_out(2, o2)
    finish_in(2, n2)

    moved = d_norm[...] * normed[...]
    in_own[...] = lane_fold(moved * gain[...])
    inner = all_col(in_own, in_in)
    folded = moved[0:8]
    for start in range(8, LOCAL, 8):
        folded = folded + moved[start : start + 8]
    gn_own[0] = folded
    gains = [send(gn_own.at[0], gn_in.at[steps - 1], at_z(steps)) for steps in (1, 2, 3)]
    arrive(gains)
    gn_own[1] = gn_own[0] + gn_in[0] + gn_in[1] + gn_in[2]
    gains = [send(gn_own.at[1], gn_in.at[steps + 2], at_y(steps)) for steps in (1, 2, 3)]
    weight_grad(token_cols(hid), act_cols(2 * UNITS), FEATS, UNITS, eu, grad_w_up, 0)
    arrive(gains)
    grad_gain[...] = jnp.sum(gn_own[1] + gn_in[3] + gn_in[4] + gn_in[5], axis=0, keepdims=True)
    arrive(inner)
    inner_all = in_own[...]
    for index in range(7):
        inner_all = inner_all + in_in[index]
    row_inner = jnp.sum(inner_all, axis=1, keepdims=True) / D
    grad_inputs[...] = (
        grad_out[...].astype(F32)
        + inv_rms[:, 0:1] * (d_norm[...] * gain[...] - normed[...] * row_inner)
    ).astype(BF16)

    for copy in started:
        copy.wait_send()


def shards(inputs, norm_gain, w_gate, w_up, w_down, mask_gate, mask_up, mask_down, grad_out):
    vmem = pl.BlockSpec(memory_space=pltpu.VMEM)
    anywhere = pl.BlockSpec(memory_space=pl.ANY)
    wide = 3 * UNITS
    shape = jax.ShapeDtypeStruct
    output, grad_inputs, grad_gain, grad_w_gate, grad_w_up, grad_w_down = pl.pallas_call(
        layer,
        out_shape=(
            shape((LOCAL, FEATS), BF16),
            shape((LOCAL, FEATS), BF16),
            shape((1, FEATS), F32),
            shape((FEATS, UNITS), BF16),
            shape((FEATS, UNITS), BF16),
            shape((UNITS, FEATS), BF16),
        ),
        in_specs=[vmem, vmem, anywhere, anywhere, anywhere, vmem, vmem, vmem, vmem],
        out_specs=(vmem, vmem, vmem, anywhere, anywhere, anywhere),
        scratch_shapes=[
            pltpu.VMEM((FEATS, UNITS), BF16),
            pltpu.VMEM((FEATS, UNITS), BF16),
            pltpu.VMEM((UNITS, FEATS), BF16),
            pltpu.VMEM((FEATS // BLOCK, SUB, UNITS), BF16),
            pltpu.VMEM((FEATS // BLOCK, SUB, UNITS), BF16),
            pltpu.VMEM((UNITS // BLOCK, SUB, FEATS), BF16),
            pltpu.VMEM((CHUNKS, 4, 4, SUB, FEATS), BF16),
            pltpu.VMEM((CHUNKS, 4, 4, SUB, FEATS), BF16),
            pltpu.VMEM((CHUNKS, 256, wide), BF16),
            pltpu.VMEM((CHUNKS, 128, wide), BF16),
            pltpu.VMEM((CHUNKS, SUB, wide), BF16),
            pltpu.VMEM((CHUNKS, SUB, wide), BF16),
            pltpu.VMEM((CHUNKS, 32, wide), BF16),
            pltpu.VMEM((CHUNKS, 32, wide), BF16),
            pltpu.VMEM((CHUNKS, 256, wide), BF16),
            pltpu.VMEM((2, CHUNKS, 4, 4, SUB, FEATS), BF16),
            pltpu.VMEM((2, CHUNKS, 3, 4, SUB, FEATS), BF16),
            pltpu.VMEM((2, CHUNKS, 4, SUB, FEATS), BF16),
            pltpu.VMEM((2, CHUNKS, 3, SUB, FEATS), BF16),
            pltpu.VMEM((LOCAL, FEATS), F32),
            pltpu.VMEM((LOCAL, 128), F32),
            pltpu.VMEM((LOCAL, FEATS), F32),
            pltpu.VMEM((LOCAL, 128), F32),
            pltpu.VMEM((7, LOCAL, 128), F32),
            pltpu.VMEM((LOCAL, 128), F32),
            pltpu.VMEM((7, LOCAL, 128), F32),
            pltpu.VMEM((2, 8, FEATS), F32),
            pltpu.VMEM((6, 8, FEATS), F32),
            pltpu.VMEM((2, TILE, UNITS), BF16),
            pltpu.VMEM((TILE, CHUNKS * 256), BF16),
            pltpu.SemaphoreType.DMA((COPIES,)),
            pltpu.SemaphoreType.DMA((COPIES,)),
            pltpu.SemaphoreType.DMA((3,)),
            pltpu.SemaphoreType.DMA((2,)),
        ],
        compiler_params=pltpu.CompilerParams(
            collective_id=0, has_side_effects=True, vmem_limit_bytes=60 << 20
        ),
        name="layer",
    )(
        inputs, norm_gain.reshape(1, FEATS), w_gate, w_up, w_down,
        mask_gate, mask_up, mask_down, grad_out,
    )
    return output, grad_inputs, grad_gain.reshape(FEATS), grad_w_gate, grad_w_up, grad_w_down


def solution(mesh):
    in_specs = (
        P("row", "col"),
        P("col"),
        P("col", "row"),
        P("col", "row"),
        P("row", "col"),
        P("col", "row"),
        P("col", "row"),
        P("row", "col"),
        P("row", "col"),
    )
    out_specs = (
        P("row", "col"),
        P("row", "col"),
        P("col"),
        P("col", "row"),
        P("col", "row"),
        P("row", "col"),
    )
    return jax.shard_map(shards, mesh=mesh, in_specs=in_specs, out_specs=out_specs, check_vma=False)
```

time: 432 us -> 163 us (0.38)
  waiting for transfers between devices: 202 us -> 0 us
  Pallas kernels: 0 us -> 145 us
  blocking collectives: 59.3 us -> 0 us
  matrix products: 58.2 us -> 0 us
  local copies, waits for them, and re-layouts: 70 us -> 15.2 us
  other arithmetic: 26 us -> 0 us
  between operations: 14 us -> 0.64 us
    pallas_call x0 -> x1, Pallas kernels: none -> 145 us  [shards(): pl.pallas_call(layer, out_shape=(shape((LOCAL, FEATS), BF16), shape((LOCA...]
    reduce_scatter x4 -> x0, waiting for transfers between devices: 130 us -> none  [the longest x1 35.6 us: shards(): lax.psum_scatter((contract_cols(d_gate_all, gate_eff) + contract_cols(d_u...]
    all_gather x5 -> x0, waiting for transfers between devices: 68.9 us -> none  [the longest x1 27.4 us: shards(): lax.all_gather(d_gate, 'col', axis=0, tiled=True)]
    psum x3 -> x0, blocking collectives: 59.3 us -> none  [the longest x1 31.7 us: shards(): grad_gain = lax.psum(gain_part, 'row')]
    dot_general x9 -> x0, matrix products: 58.2 us -> none  [the longest x3 23.6 us: contract_cols(): lax.dot_general(left, right, (((1,), (1,)), ((), ())), preferred_element_...]
    mul x9 -> x0, local copies, waits for them, and re-layouts: 55.9 us -> none  [the longest x8 55.9 us: expand_mask(): weight.reshape(mask_rows, BLOCK, mask_cols, BLOCK)]
    mul x4 -> x0, other arithmetic: 12.7 us -> none  [the longest x2 10.8 us: expand_mask(): weight.reshape(mask_rows, BLOCK, mask_cols, BLOCK)]
    convert_element_type x7 -> x0, other arithmetic: 7.48 us -> none  [the longest x1 2.29 us: shards(): d_up = (d_hidden * silu_gate).astype(jnp.bfloat16)]
  transfers between devices with their start and end apart: 9 -> 0, of which waited for: 7 -> 0; matrix products, arithmetic and copies ran while one was open for 34% -> 0% of each run, Pallas kernels for 0% -> 0%
where the time goes in v1:
time: 163 us; the launch traced here: 161 us
  Pallas kernels  145 us (89%)
  local copies, waits for them, and re-layouts  15.2 us (9%)
    pallas_call x1, Pallas kernels, shards(): pl.pallas_call(layer, out_shape=(shape((LOCAL, FEATS), BF16), shape((LOCA...  145 us
    unnamed x11, local copies, waits for them, and re-layouts  15.2 us

profile of v1, /device:TPU:1, one launch (start us, length us, event | category | flops | bytes accessed | tf_op | source)
XLA Modules:
  0.0 161.2 jit_solution(7452349018006313999)
XLA Ops:
  0.6 1.4 copy.15.mask_down
  2.0 145.4 %layer.1 = (bf16[48,1024]{1,0:T(8,128)(2,1)}, bf16[48,1024]{1,0:T(8,128)(2,1)}, f32[1,1024]{1,0:T(1,128)}, bf16[1024,1792]{1,0:T(8,128)(2,1)}, bf16[1024,1792]{1,0:T(8,128)(2,1)}, /*index=5*/bf16[1792,1024]{1,0:T(8,128)(2,1)}) custom-call(bf16[48,1024]{1,0:T(8,128)(2,1)} %inputs.1, f32[1,1024]{1,0:T(1,128)} %bitcast.2, bf16[1024,1792]{1,0:T(8,128)(2,1)} %w_gate.1, ...), custom_call_target="tpu_custom_call" | custom-call | tf_op jit(solution)/shard_map/layer/pallas_call | solution.py:517
  147.4 1.5 copy.22
  149.0 1.5 copy.23
  150.5 1.3 copy.24
  151.8 0.0 copy-start.1
  151.8 4.3 %copy.25 = bf16[1024,1792]{1,0:T(8,128)(2,1)} copy(bf16[1024,1792]{1,0:T(8,128)(2,1)} %get-tuple-element.27) | data formatting | bytes 7340032
  156.0 0.0 copy-done.1
  156.0 0.0 copy-start
  156.0 1.9 %copy.26 = bf16[1024,1792]{1,0:T(8,128)(2,1)} copy(bf16[1024,1792]{1,0:T(8,128)(2,1)S(1)} %copy-done.1) | data formatting | bytes 7340032
  157.9 1.5 copy-done
  159.4 1.8 %copy.27 = bf16[1792,1024]{1,0:T(8,128)(2,1)} copy(bf16[1792,1024]{1,0:T(8,128)(2,1)S(1)} %copy-done) | data formatting | bytes 7340032
Async XLA Ops:
  151.8 4.3 %copy-start.1 = (bf16[1024,1792]{1,0:T(8,128)(2,1)S(1)}, bf16[1024,1792]{1,0:T(8,128)(2,1)}, u32[]{:S(2)}) copy-start(bf16[1024,1792]{1,0:T(8,128)(2,1)} %get-tuple-element.28) | copy-start | bytes 11010052
  156.0 3.4 %copy-start = (bf16[1792,1024]{1,0:T(8,128)(2,1)S(1)}, bf16[1792,1024]{1,0:T(8,128)(2,1)}, u32[]{:S(2)}) copy-start(bf16[1792,1024]{1,0:T(8,128)(2,1)} %get-tuple-element.29) | copy-start | bytes 11010052

commit v2 on v1

v2 whole, which is shorter than its diff:
```python
import functools

import jax
import jax.numpy as jnp
from jax import lax
from jax.experimental import pallas as pl
from jax.experimental.pallas import tpu as pltpu
from jax.sharding import PartitionSpec as P

D = 8192
BLOCK = 64
EPSILON = 1e-05
MESH = pl.DeviceIdType.MESH
F32 = jnp.float32
BF16 = jnp.bfloat16

LOCAL = 48
CHUNKS = 3
SUB = 16
FEATS = 1024
UNITS = 1792
HALF = FEATS // 2
TILE = 256
COPIES = 320


def nt_dot(left, right):
    return lax.dot_general(left, right, (((1,), (1,)), ((), ())), preferred_element_type=F32)


def nn_dot(left, right):
    return lax.dot_general(left, right, (((1,), (0,)), ((), ())), preferred_element_type=F32)


def tn_dot(left, right):
    return lax.dot_general(left, right, (((0,), (0,)), ((), ())), preferred_element_type=F32)


def masked(product, wide_mask):
    rows, width = product.shape
    blocks = product.astype(BF16).reshape(rows // BLOCK, BLOCK // SUB, SUB, width)
    return (blocks * wide_mask.reshape(rows // BLOCK, 1, SUB, width)).reshape(rows, width)


def lane_fold(value):
    total = value[:, 0:128]
    for start in range(128, value.shape[1], 128):
        total = total + value[:, start : start + 128]
    return total


def widen(mask, into):
    rows, blocks = mask.shape
    width = blocks * BLOCK
    unit = lax.broadcasted_iota(jnp.int32, (blocks, width), 1)
    first = lax.broadcasted_iota(jnp.int32, (blocks, width), 0) * BLOCK
    spread = jnp.where((unit >= first) & (unit < first + BLOCK), 1.0, 0.0).astype(BF16)
    wide_mask = nn_dot(mask.astype(F32).astype(BF16), spread)
    for r in range(rows):
        into[r] = jnp.broadcast_to(wide_mask[r : r + 1, :], (SUB, width)).astype(BF16)


def layer(
    inputs, gain, w_gate, w_up, w_down, mask_gate, mask_up, mask_down, grad_out,
    output, grad_inputs, grad_gain, grad_w_gate, grad_w_down, d_up_all, hid_all,
    wg, wu, wd, eg, eu, ed, hid, cot, part, pair, fwd_a, fwd_b, from_l, from_r, act,
    row_part, row_in1, row_sum, row_in2, normed, inv_rms, d_norm,
    sq_own, sq_in, in_own, in_in, gn_own, gn_in, stage_d, stage_u,
    send_sem, recv_sem, load_sem, store_sem, keep_sem,
):
    row = lax.axis_index("row")
    col = lax.axis_index("col")
    y, z = row // 4, lax.rem(row, 4)
    x, core = col // 2, lax.rem(col, 2)

    def up(value, steps):
        return lax.rem(value + steps, 4)

    def at_x(steps, other=0):
        return (row, up(x, steps) * 2 + (1 - core if other else core))

    def at_y(steps):
        return (up(y, steps) * 4 + z, col)

    def at_z(steps):
        return (y * 4 + up(z, steps), col)

    partner = at_x(0, 1)
    started = []

    def send(src, dst, device):
        index = len(started)
        copy = pltpu.make_async_remote_copy(
            src_ref=src, dst_ref=dst, send_sem=send_sem.at[index], recv_sem=recv_sem.at[index],
            device_id=device, device_id_type=MESH,
        )
        copy.start()
        started.append(copy)
        return copy

    kept = []

    def keep(source, target):
        copy = pltpu.make_async_copy(source, target, keep_sem.at[len(kept)])
        copy.start()
        kept.append(copy)

    def arrive(copies):
        for copy in copies:
            copy.wait_recv()

    loads = [
        pltpu.make_async_copy(source, target, load_sem.at[index])
        for index, (source, target) in enumerate(((w_down, wd), (w_gate, wg), (w_up, wu)))
    ]
    for load in loads:
        load.start()

    barrier = pltpu.get_barrier_semaphore()
    row_peers = [
        (up(y, steps // 4) * 4 + up(z, steps % 4), col) for steps in range(1, 16)
    ]
    neighbours = [partner] + row_peers
    for steps in (1, 2, 3):
        neighbours += [at_x(steps), at_x(steps, 1)]
    for device in neighbours:
        pl.semaphore_signal(barrier, inc=1, device_id=device, device_id_type=MESH)

    for k in range(CHUNKS):
        cot[k, y, z] = grad_out[k * SUB : (k + 1) * SUB, :]
    wide = inputs[...].astype(F32)
    sq_own[...] = lane_fold(wide * wide)

    pl.semaphore_wait(barrier, len(neighbours))

    def all_col(own, into):
        copies = [send(own, into.at[0], partner)]
        for steps in (1, 2, 3):
            copies.append(send(own, into.at[2 * steps - 1], at_x(steps)))
            copies.append(send(own, into.at[2 * steps], at_x(steps, 1)))
        return copies

    def gather1(ref, k):
        copies = []
        for steps in (1, 2, 3):
            part_a = ref.at[k, y, z, :, pl.ds(0, HALF)]
            part_b = ref.at[k, y, z, :, pl.ds(HALF, HALF)]
            copies.append(send(part_a, part_a, at_z(steps)))
            copies.append(send(part_b, part_b, at_y(steps)))
        return copies

    def gather2(ref, k):
        copies = []
        for steps in (1, 2, 3):
            part_a = ref.at[k, y, :, :, pl.ds(0, HALF)]
            part_b = ref.at[k, :, z, :, pl.ds(HALF, HALF)]
            copies.append(send(part_a, part_a, at_y(steps)))
            copies.append(send(part_b, part_b, at_z(steps)))
        return copies

    cot1 = [gather1(cot, 0)]
    squares = all_col(sq_own, sq_in)

    def mask_weights(ref, wide_mask, load):
        load.wait()

        def body(r, carry):
            kept = wide_mask[r]
            for piece in range(BLOCK // SUB):
                rows = pl.ds(pl.multiple_of(r * BLOCK + piece * SUB, SUB), SUB)
                ref[rows, :] = ref[rows, :] * kept
            return carry

        lax.fori_loop(0, wide_mask.shape[0], body, 0)

    widen(mask_down[...].astype(F32).T, ed)
    mask_weights(wd, ed, loads[0])
    arrive(cot1[0])
    cot2 = [gather2(cot, 0)]

    arrive(squares)
    squares_all = sq_own[...]
    for index in range(7):
        squares_all = squares_all + sq_in[index]
    inv_rms[...] = jnp.broadcast_to(
        lax.rsqrt(jnp.sum(squares_all, axis=1, keepdims=True) / D + EPSILON), (LOCAL, 128)
    )
    normed[...] = inputs[...].astype(F32) * inv_rms[:, 0:1]
    own_hidden_in = (normed[...] * gain[...]).astype(BF16)
    for k in range(CHUNKS):
        hid[k, y, z] = own_hidden_in[k * SUB : (k + 1) * SUB, :]
    hid1 = [gather1(hid, 0)]
    widen(mask_gate[...], eg)
    mask_weights(wg, eg, loads[1])
    arrive(hid1[0])
    hid2 = [gather2(hid, 0)]
    for k in (1, 2):
        cot1.append(gather1(cot, k))
        hid1.append(gather1(hid, k))
    widen(mask_up[...], eu)
    mask_weights(wu, eu, loads[2])

    def chunk_of(ref, k):
        return ref[k].reshape(4 * 4 * SUB, FEATS)

    def tiles(count, body):
        def step(n, carry):
            body(pl.multiple_of(n * TILE, TILE))
            return carry

        lax.fori_loop(0, count, step, 0)

    def pair_send(k, start, width):
        return [
            send(
                part.at[k, pl.ds(pl.multiple_of((1 - core) * 128, 128), 128), pl.ds(start, width)],
                pair.at[k, :, pl.ds(start, width)],
                partner,
            )
        ]

    def mm_down_back(k):
        arrive(cot2[k])
        copies = []
        for start in (0, UNITS // 2):
            rows = slice(start, start + UNITS // 2)
            part[k, :, rows] = nt_dot(chunk_of(cot, k), wd[rows, :]).astype(BF16)
            copies += pair_send(k, start, UNITS // 2)
        return copies

    def mm_gate(k):
        arrive(hid2[k])
        part[k, :, UNITS : 2 * UNITS] = nn_dot(chunk_of(hid, k), wg[...]).astype(BF16)
        return pair_send(k, UNITS, UNITS)

    def mm_up(k):
        part[k, :, 2 * UNITS : 3 * UNITS] = nn_dot(chunk_of(hid, k), wu[...]).astype(BF16)
        return pair_send(k, 2 * UNITS, UNITS)

    def block_rows(which, offset, count):
        return pl.ds(pl.multiple_of(which * 32 + offset, SUB), count)

    def scatter1(k, job, copies):
        start, width = job
        cols = pl.ds(start, width)
        arrive(copies)
        mine = pl.multiple_of(core * 128, 128)
        def body(r, carry):
            rows = pl.ds(pl.multiple_of(r * SUB, SUB), SUB)
            own = part[k, pl.ds(pl.multiple_of(mine + r * SUB, SUB), SUB), cols].astype(F32)
            pair[k, rows, cols] = (own + pair[k, rows, cols].astype(F32)).astype(BF16)
            return carry
        lax.fori_loop(0, 8, body, 0)
        right, left = at_x(1), at_x(3)
        two = up(x, 2)
        return (
            send(pair.at[k, block_rows(two, 0, SUB), cols], fwd_a.at[k, :, cols], right),
            send(pair.at[k, block_rows(two, SUB, SUB), cols], fwd_b.at[k, :, cols], left),
            send(pair.at[k, block_rows(up(x, 1), SUB, SUB), cols], from_l.at[k, pl.ds(SUB, SUB), cols], right),
            send(pair.at[k, block_rows(up(x, 3), 0, SUB), cols], from_r.at[k, pl.ds(0, SUB), cols], left),
        )

    def scatter2(k, job, copies):
        start, width = job
        cols = pl.ds(start, width)
        right, left = at_x(1), at_x(3)
        arrive(copies[0:1])
        own = pair[k, block_rows(up(x, 1), 0, SUB), cols].astype(F32)
        fwd_a[k, :, cols] = (own + fwd_a[k, :, cols].astype(F32)).astype(BF16)
        first = send(fwd_a.at[k, :, cols], from_l.at[k, pl.ds(0, SUB), cols], right)
        arrive(copies[1:2])
        own = pair[k, block_rows(up(x, 3), SUB, SUB), cols].astype(F32)
        fwd_b[k, :, cols] = (own + fwd_b[k, :, cols].astype(F32)).astype(BF16)
        second = send(fwd_b.at[k, :, cols], from_r.at[k, pl.ds(SUB, SUB), cols], left)
        return (copies[2], copies[3], first, second)

    down_job, gate_up_job = (0, UNITS), (UNITS, 2 * UNITS)
    gate_job, up_job = (UNITS, UNITS), (2 * UNITS, UNITS)
    owner = core * 4 + x

    def activate(k, copies):
        arrive(copies)
        def total(start):
            cols = pl.ds(start, 256)
            return (
                pair[k, block_rows(x, 0, 32), cols].astype(F32)
                + from_l[k, :, cols].astype(F32)
                + from_r[k, :, cols].astype(F32)
            )

        def body(at):
            d_hidden = total(at)
            gate_value = total(UNITS + at)
            up_value = total(2 * UNITS + at)
            sigma = jax.nn.sigmoid(gate_value)
            silu = gate_value * sigma
            rows = block_rows(owner, 0, 32)
            act[k, rows, pl.ds(at, 256)] = (silu * up_value).astype(BF16)
            act[k, rows, pl.ds(UNITS + at, 256)] = (
                d_hidden * up_value * sigma * (1.0 + gate_value * (1.0 - sigma))
            ).astype(BF16)
            act[k, rows, pl.ds(2 * UNITS + at, 256)] = (d_hidden * silu).astype(BF16)

        tiles(UNITS // 256, body)

    def spread1(k, job):
        block = act.at[k, block_rows(owner, 0, 32), pl.ds(*job)]
        return (
            send(block, block, at_x(1)),
            send(block, block, at_x(3)),
            send(block, block, partner),
        )

    def spread2(k, job, copies):
        cols = pl.ds(*job)
        from_left, from_right = core * 4 + up(x, 3), core * 4 + up(x, 1)
        arrive(copies[0:1])
        half = act.at[k, block_rows(from_left, 0, SUB), cols]
        block = act.at[k, block_rows(from_left, 0, 32), cols]
        first = send(half, half, at_x(1))
        first_pair = send(block, block, partner)
        arrive(copies[1:2])
        half = act.at[k, block_rows(from_right, SUB, SUB), cols]
        block = act.at[k, block_rows(from_right, 0, 32), cols]
        second = send(half, half, at_x(3))
        second_pair = send(block, block, partner)
        return (first, second), (copies[2], first_pair, second_pair)

    def spread3(k, job, halves, pairs):
        arrive(halves)
        block = act.at[k, block_rows(core * 4 + up(x, 2), 0, 32), pl.ds(*job)]
        return pairs + (send(block, block, partner),)

    halves = (slice(0, HALF), slice(HALF, FEATS))

    def row_scatter1(which, k, half):
        copies = []
        lanes = pl.ds(half * HALF, HALF)
        for steps in (1, 2, 3):
            into = row_in1.at[which, k, steps - 1, :, :, lanes]
            if half == 0:
                copies.append(send(row_part.at[which, k, up(y, steps), :, :, lanes], into, at_y(steps)))
            else:
                copies.append(send(row_part.at[which, k, :, up(z, steps), :, lanes], into, at_z(steps)))
        return copies

    def row_scatter2(which, k, half, copies):
        arrive(copies)
        lanes = halves[half]
        if half == 0:
            total = row_part[which, k, y, :, :, lanes].astype(F32)
        else:
            total = row_part[which, k, :, z, :, lanes].astype(F32)
        for index in range(3):
            total = total + row_in1[which, k, index, :, :, lanes].astype(F32)
        row_sum[which, k, :, :, lanes] = total.astype(BF16)
        after = []
        lanes = pl.ds(half * HALF, HALF)
        for steps in (1, 2, 3):
            into = row_in2.at[which, k, steps - 1, :, lanes]
            if half == 0:
                after.append(send(row_sum.at[which, k, up(z, steps), :, lanes], into, at_z(steps)))
            else:
                after.append(send(row_sum.at[which, k, up(y, steps), :, lanes], into, at_y(steps)))
        return after

    def row_scatters2(which, k, copies):
        return row_scatter2(which, k, 0, copies[0:3]) + row_scatter2(which, k, 1, copies[3:6])

    def row_total(which, k, half):
        lanes = halves[half]
        total = row_sum[which, k, y if half else z, :, lanes].astype(F32)
        for index in range(3):
            total = total + row_in2[which, k, index, :, lanes].astype(F32)
        return total

    def mm_out(k, pairs):
        arrive(pairs)
        product = nn_dot(act[k, :, 0:UNITS], wd[...]).astype(BF16)
        row_part[0, k] = product.reshape(4, 4, SUB, FEATS)
        return row_scatter1(0, k, 0) + row_scatter1(0, k, 1)

    def mm_in_back(k, pairs):
        arrive(pairs)
        keep(act.at[k, :, pl.ds(2 * UNITS, UNITS)], d_up_all.at[k])
        copies = []
        for half, lanes in enumerate(halves):
            product = nt_dot(act[k, :, UNITS : 2 * UNITS], wg[lanes, :]) + nt_dot(
                act[k, :, 2 * UNITS : 3 * UNITS], wu[lanes, :]
            )
            row_part[1, k, :, :, :, lanes] = product.astype(BF16).reshape(4, 4, SUB, HALF)
            copies += row_scatter1(1, k, half)
        return copies

    def finish_out(k, copies):
        arrive(copies)
        rows = slice(k * SUB, (k + 1) * SUB)
        for half, lanes in enumerate(halves):
            output[rows, lanes] = (inputs[rows, lanes].astype(F32) + row_total(0, k, half)).astype(BF16)

    def finish_in(k, copies):
        arrive(copies)
        rows = slice(k * SUB, (k + 1) * SUB)
        for half, lanes in enumerate(halves):
            d_norm[rows, lanes] = row_total(1, k, half)

    def weight_grad(left_of, right, wide_mask, target, stage, sems, first, last, reuse):
        def body(m, carry):
            at = pl.multiple_of(m * TILE, TILE)
            use = lax.rem(m, 2)

            def store():
                return pltpu.make_async_copy(stage.at[use], target.at[pl.ds(at, TILE), :], sems.at[use])

            if reuse:
                store().wait()
            else:
                @pl.when(m >= 2)
                def _():
                    store().wait()

            stage[use] = masked(tn_dot(left_of(at), right()), wide_mask[pl.ds(m * 4, 4)])
            store().start()
            return carry

        lax.fori_loop(first, last, body, 0)

    tokens = CHUNKS * 256

    def grad_down(first, last, reuse):
        weight_grad(
            lambda at: act[:, :, pl.ds(at, TILE)].reshape(tokens, TILE),
            lambda: cot[...].reshape(tokens, FEATS),
            ed, grad_w_down, stage_d, store_sem.at[0], first, last, reuse,
        )

    def grad_gate(first, last, reuse):
        weight_grad(
            lambda at: hid[:, :, :, :, pl.ds(at, TILE)].reshape(tokens, TILE),
            lambda: act[:, :, UNITS : 2 * UNITS].reshape(tokens, UNITS),
            eg, grad_w_gate, stage_u, store_sem.at[1], first, last, reuse,
        )

    all_job, out_job, in_job = (0, 3 * UNITS), (0, UNITS), (UNITS, 2 * UNITS)
    pd0 = mm_down_back(0)
    arrive(cot1[1])
    cot2.append(gather2(cot, 1))
    sd0 = scatter1(0, down_job, pd0)
    pg0 = mm_gate(0)
    pu0 = mm_up(0)
    arrive(hid1[1])
    hid2.append(gather2(hid, 1))
    sg0 = scatter1(0, gate_job, pg0)
    td0 = scatter2(0, down_job, sd0)
    su0 = scatter1(0, up_job, pu0)
    arrive(cot1[2])
    cot2.append(gather2(cot, 2))
    arrive(hid1[2])
    hid2.append(gather2(hid, 2))
    pd1 = mm_down_back(1)
    tg0 = scatter2(0, gate_job, sg0)
    pg1 = mm_gate(1) + mm_up(1)
    tu0 = scatter2(0, up_job, su0)
    sd1 = scatter1(1, down_job, pd1)
    sg1 = scatter1(1, gate_up_job, pg1)
    pd2 = mm_down_back(2)
    pg2 = mm_gate(2) + mm_up(2)
    for k in range(CHUNKS):
        keep(hid.at[k], hid_all.at[k])
    td1 = scatter2(1, down_job, sd1)
    activate(0, td0 + tg0 + tu0)
    a0 = spread1(0, all_job)
    sd2 = scatter1(2, down_job, pd2)
    tg1 = scatter2(1, gate_up_job, sg1)
    sg2 = scatter1(2, gate_up_job, pg2)
    h0, q0 = spread2(0, all_job, a0)
    activate(1, td1 + tg1)
    a1 = spread1(1, all_job)
    td2 = scatter2(2, down_job, sd2)
    r0 = spread3(0, all_job, h0, q0)
    tg2 = scatter2(2, gate_up_job, sg2)
    h1, q1 = spread2(1, all_job, a1)
    n0 = mm_in_back(0, r0)
    o0 = mm_out(0, ())
    activate(2, td2 + tg2)
    a2 = spread1(2, in_job)
    b2 = spread1(2, out_job)
    r1 = spread3(1, all_job, h1, q1)
    n0 = row_scatters2(1, 0, n0)
    o0 = row_scatters2(0, 0, o0)
    h2, q2 = spread2(2, in_job, a2)
    u2, v2 = spread2(2, out_job, b2)
    n1 = mm_in_back(1, r1)
    o1 = mm_out(1, ())
    finish_out(0, o0)
    finish_in(0, n0)
    r2 = spread3(2, in_job, h2, q2)
    n1 = row_scatters2(1, 1, n1)
    o1 = row_scatters2(0, 1, o1)
    n2 = mm_in_back(2, r2)
    w2 = spread3(2, out_job, u2, v2)
    finish_out(1, o1)
    finish_in(1, n1)
    grad_gate(0, 1, False)
    o2 = mm_out(2, w2)
    n2 = row_scatters2(1, 2, n2)
    grad_gate(1, 2, False)
    o2 = row_scatters2(0, 2, o2)
    finish_in(2, n2)

    moved = d_norm[...] * normed[...]
    in_own[...] = lane_fold(moved * gain[...])
    inner = all_col(in_own, in_in)
    gn_own[...] = jnp.sum(moved, axis=0, keepdims=True)
    gains = [send(gn_own, gn_in.at[index], device) for index, device in enumerate(row_peers)]
    grad_gate(2, 4, True)
    finish_out(2, o2)
    grad_down(0, 1, False)
    arrive(inner)
    inner_all = in_own[...]
    for index in range(7):
        inner_all = inner_all + in_in[index]
    row_inner = jnp.sum(inner_all, axis=1, keepdims=True) / D
    grad_inputs[...] = (
        grad_out[...].astype(F32)
        + inv_rms[:, 0:1] * (d_norm[...] * gain[...] - normed[...] * row_inner)
    ).astype(BF16)
    arrive(gains)
    gain_total = gn_own[...]
    for index in range(15):
        gain_total = gain_total + gn_in[index]
    grad_gain[...] = gain_total
    grad_down(1, 7, False)
    for use in range(2):
        pltpu.make_async_copy(stage_d.at[use], grad_w_down.at[pl.ds(0, TILE), :], store_sem.at[0, use]).wait()
        pltpu.make_async_copy(stage_u.at[use], grad_w_gate.at[pl.ds(0, TILE), :], store_sem.at[1, use]).wait()
    for copy in kept:
        copy.wait()
    for copy in started:
        copy.wait_send()


def last_grad(
    output_in, grad_inputs_in, grad_gain_in, grad_w_gate_in, grad_w_down_in, d_up_all, hid_all, mask_up,
    output, grad_inputs, grad_gain, grad_w_gate, grad_w_up, grad_w_down,
    d_up, hid, eu, small_a, small_b, small_c, big_a, big_b, stage, need_sem, in_sem, out_sem,
):
    needs = [
        pltpu.make_async_copy(d_up_all, d_up, need_sem.at[0]),
        pltpu.make_async_copy(hid_all, hid, need_sem.at[1]),
    ]
    for need in needs:
        need.start()
    moves = [
        (output_in, small_a, output, slice(0, LOCAL)),
        (grad_inputs_in, small_b, grad_inputs, slice(0, LOCAL)),
        (grad_gain_in, small_c, grad_gain, slice(0, 1)),
    ]
    for source, held, target in ((grad_w_gate_in, big_a, grad_w_gate), (grad_w_down_in, big_b, grad_w_down)):
        rows = source.shape[0] // 4
        moves += [(source, held, target, slice(n * rows, (n + 1) * rows)) for n in range(4)]
    loads, saves = [], []
    for index, (source, held, target, rows) in enumerate(moves):
        loads.append(pltpu.make_async_copy(source.at[rows, :], held.at[rows, :], in_sem.at[index]))
        loads[-1].start()

    def move(count):
        for _ in range(count):
            index = len(saves)
            source, held, target, rows = moves[index]
            loads[index].wait()
            saves.append(pltpu.make_async_copy(held.at[rows, :], target.at[rows, :], out_sem.at[index]))
            saves[-1].start()

    widen(mask_up[...], eu)
    for need in needs:
        need.wait()
    grads = []
    tokens = CHUNKS * 256
    for m in range(FEATS // TILE):
        rows = slice(m * TILE, (m + 1) * TILE)
        product = tn_dot(
            hid[:, :, :, :, rows].reshape(tokens, TILE), d_up[...].reshape(tokens, UNITS)
        )
        stage[m] = masked(product, eu[m * 4 : (m + 1) * 4])
        grads.append(pltpu.make_async_copy(stage.at[m], grad_w_up.at[rows, :], need_sem.at[m + 2]))
        grads[-1].start()
        move((2, 3, 3, 3)[m])
    for copy in saves + grads:
        copy.wait()


def shards(inputs, norm_gain, w_gate, w_up, w_down, mask_gate, mask_up, mask_down, grad_out):
    vmem = pl.BlockSpec(memory_space=pltpu.VMEM)
    anywhere = pl.BlockSpec(memory_space=pl.ANY)
    wide = 3 * UNITS
    shape = jax.ShapeDtypeStruct
    results = pl.pallas_call(
        layer,
        out_shape=(
            shape((LOCAL, FEATS), BF16),
            shape((LOCAL, FEATS), BF16),
            shape((1, FEATS), F32),
            shape((FEATS, UNITS), BF16),
            shape((UNITS, FEATS), BF16),
            shape((CHUNKS, 256, UNITS), BF16),
            shape((CHUNKS, 4, 4, SUB, FEATS), BF16),
        ),
        in_specs=[vmem, vmem, anywhere, anywhere, anywhere, vmem, vmem, vmem, vmem],
        out_specs=(vmem, vmem, vmem, anywhere, anywhere, anywhere, anywhere),
        scratch_shapes=[
            pltpu.VMEM((FEATS, UNITS), BF16),
            pltpu.VMEM((FEATS, UNITS), BF16),
            pltpu.VMEM((UNITS, FEATS), BF16),
            pltpu.VMEM((FEATS // BLOCK, SUB, UNITS), BF16),
            pltpu.VMEM((FEATS // BLOCK, SUB, UNITS), BF16),
            pltpu.VMEM((UNITS // BLOCK, SUB, FEATS), BF16),
            pltpu.VMEM((CHUNKS, 4, 4, SUB, FEATS), BF16),
            pltpu.VMEM((CHUNKS, 4, 4, SUB, FEATS), BF16),
            pltpu.VMEM((CHUNKS, 256, wide), BF16),
            pltpu.VMEM((CHUNKS, 128, wide), BF16),
            pltpu.VMEM((CHUNKS, SUB, wide), BF16),
            pltpu.VMEM((CHUNKS, SUB, wide), BF16),
            pltpu.VMEM((CHUNKS, 32, wide), BF16),
            pltpu.VMEM((CHUNKS, 32, wide), BF16),
            pltpu.VMEM((CHUNKS, 256, wide), BF16),
            pltpu.VMEM((2, CHUNKS, 4, 4, SUB, FEATS), BF16),
            pltpu.VMEM((2, CHUNKS, 3, 4, SUB, FEATS), BF16),
            pltpu.VMEM((2, CHUNKS, 4, SUB, FEATS), BF16),
            pltpu.VMEM((2, CHUNKS, 3, SUB, FEATS), BF16),
            pltpu.VMEM((LOCAL, FEATS), F32),
            pltpu.VMEM((LOCAL, 128), F32),
            pltpu.VMEM((LOCAL, FEATS), F32),
            pltpu.VMEM((LOCAL, 128), F32),
            pltpu.VMEM((7, LOCAL, 128), F32),
            pltpu.VMEM((LOCAL, 128), F32),
            pltpu.VMEM((7, LOCAL, 128), F32),
            pltpu.VMEM((1, FEATS), F32),
            pltpu.VMEM((15, 1, FEATS), F32),
            pltpu.VMEM((2, TILE, FEATS), BF16),
            pltpu.VMEM((2, TILE, UNITS), BF16),
            pltpu.SemaphoreType.DMA((COPIES,)),
            pltpu.SemaphoreType.DMA((COPIES,)),
            pltpu.SemaphoreType.DMA((3,)),
            pltpu.SemaphoreType.DMA((2, 2)),
            pltpu.SemaphoreType.DMA((2 * CHUNKS,)),
        ],
        compiler_params=pltpu.CompilerParams(
            collective_id=0, has_side_effects=True, vmem_limit_bytes=60 << 20
        ),
        name="layer",
    )(
        inputs, norm_gain.reshape(1, FEATS), w_gate, w_up, w_down,
        mask_gate, mask_up, mask_down.T, grad_out,
    )
    output, grad_inputs, grad_gain, grad_w_gate, grad_w_up, grad_w_down = pl.pallas_call(
        last_grad,
        out_shape=(
            shape((LOCAL, FEATS), BF16),
            shape((LOCAL, FEATS), BF16),
            shape((1, FEATS), F32),
            shape((FEATS, UNITS), BF16),
            shape((FEATS, UNITS), BF16),
            shape((UNITS, FEATS), BF16),
        ),
        in_specs=[anywhere] * 7 + [vmem],
        out_specs=(anywhere,) * 6,
        scratch_shapes=[
            pltpu.VMEM((CHUNKS, 256, UNITS), BF16),
            pltpu.VMEM((CHUNKS, 4, 4, SUB, FEATS), BF16),
            pltpu.VMEM((FEATS // BLOCK, SUB, UNITS), BF16),
            pltpu.VMEM((LOCAL, FEATS), BF16),
            pltpu.VMEM((LOCAL, FEATS), BF16),
            pltpu.VMEM((1, FEATS), F32),
            pltpu.VMEM((FEATS, UNITS), BF16),
            pltpu.VMEM((UNITS, FEATS), BF16),
            pltpu.VMEM((4, TILE, UNITS), BF16),
            pltpu.SemaphoreType.DMA((6,)),
            pltpu.SemaphoreType.DMA((11,)),
            pltpu.SemaphoreType.DMA((11,)),
        ],
        compiler_params=pltpu.CompilerParams(vmem_limit_bytes=60 << 20),
        name="last_grad",
    )(*results, mask_up)
    return output, grad_inputs, grad_gain.reshape(FEATS), grad_w_gate, grad_w_up, grad_w_down


def solution(mesh):
    in_specs = (
        P("row", "col"),
        P("col"),
        P("col", "row"),
        P("col", "row"),
        P("row", "col"),
        P("col", "row"),
        P("col", "row"),
        P("row", "col"),
        P("row", "col"),
    )
    out_specs = (
        P("row", "col"),
        P("row", "col"),
        P("col"),
        P("col", "row"),
        P("col", "row"),
        P("row", "col"),
    )
    return jax.shard_map(shards, mesh=mesh, in_specs=in_specs, out_specs=out_specs, check_vma=False)
```

time: 163 us -> 142 us (0.87)
  local copies, waits for them, and re-layouts: 15.2 us -> 0 us
  Pallas kernels: 145 us -> 141 us
    pallas_call x1, Pallas kernels: 145 us -> 130 us  [shards(): pl.pallas_call(layer, out_shape=(shape((LOCAL, FEATS), BF16), shape((LOCA...]
    unnamed x11 -> x0, local copies, waits for them, and re-layouts: 15.2 us -> none
    pallas_call x0 -> x1, Pallas kernels: none -> 11.2 us  [shards(): pl.pallas_call(last_grad, out_shape=(shape((LOCAL, FEATS), BF16), shape((...]
where the time goes in v2:
time: 142 us
  Pallas kernels  141 us (99%)
    pallas_call x1, Pallas kernels, shards(): pl.pallas_call(layer, out_shape=(shape((LOCAL, FEATS), BF16), shape((LOCA...  130 us
    pallas_call x1, Pallas kernels, shards(): pl.pallas_call(last_grad, out_shape=(shape((LOCAL, FEATS), BF16), shape((...  11.2 us

profile of v2, /device:TPU:1, one launch (start us, length us, event | category | flops | bytes accessed | tf_op | source)
XLA Modules:
  0.0 141.5 jit_solution(1217164131596844966)
XLA Ops:
  0.6 129.6 %layer.1 = (bf16[48,1024]{1,0:T(8,128)(2,1)}, bf16[48,1024]{1,0:T(8,128)(2,1)}, f32[1,1024]{1,0:T(1,128)}, bf16[1024,1792]{1,0:T(8,128)(2,1)}, bf16[1792,1024]{1...) custom-call(bf16[48,1024]{1,0:T(8,128)(2,1)} %inputs.1, f32[1,1024]{1,0:T(1,128)} %bitcast.4, ...), custom_call_target="tpu_custom_call" | custom-call | tf_op jit(solution)/shard_map/layer/pallas_call | solution.py:598
  130.2 11.2 %last_grad.1 = (bf16[48,1024]{1,0:T(8,128)(2,1)}, bf16[48,1024]{1,0:T(8,128)(2,1)}, f32[1,1024]{1,0:T(1,128)}, bf16[1024,1792]{1,0:T(8,128)(2,1)}, bf16[1024,179...) custom-call(bf16[48,1024]{1,0:T(8,128)(2,1)} %get-tuple-element.19.output_in, ...), custom_call_target="tpu_custom_call" | custom-call | tf_op jit(solution)/shard_map/last_grad/pallas_call | solution.py:656

commit v3 on v2

--- a/solution.py
+++ b/solution.py
@@ -63,7 +63,7 @@
 def layer(
     inputs, gain, w_gate, w_up, w_down, mask_gate, mask_up, mask_down, grad_out,
     output, grad_inputs, grad_gain, grad_w_gate, grad_w_down, d_up_all, hid_all,
-    wg, wu, wd, eg, eu, ed, hid, cot, part, pair, fwd_a, fwd_b, from_l, from_r, act,
+    gate_early, down_early, wg, wu, wd, eg, eu, ed, hid, cot, part, pair, fwd_a, fwd_b, from_l, from_r, act,
     row_part, row_in1, row_sum, row_in2, normed, inv_rms, d_norm,
     sq_own, sq_in, in_own, in_in, gn_own, gn_in, stage_d, stage_u,
     send_sem, recv_sem, load_sem, store_sem, keep_sem,
@@ -174,7 +174,6 @@
         lax.fori_loop(0, wide_mask.shape[0], body, 0)
 
     widen(mask_down[...].astype(F32).T, ed)
-    mask_weights(wd, ed, loads[0])
     arrive(cot1[0])
     cot2 = [gather2(cot, 0)]
 
@@ -185,20 +184,22 @@
     inv_rms[...] = jnp.broadcast_to(
         lax.rsqrt(jnp.sum(squares_all, axis=1, keepdims=True) / D + EPSILON), (LOCAL, 128)
     )
-    normed[...] = inputs[...].astype(F32) * inv_rms[:, 0:1]
-    own_hidden_in = (normed[...] * gain[...]).astype(BF16)
+    hid1 = []
     for k in range(CHUNKS):
-        hid[k, y, z] = own_hidden_in[k * SUB : (k + 1) * SUB, :]
-    hid1 = [gather1(hid, 0)]
-    widen(mask_gate[...], eg)
-    mask_weights(wg, eg, loads[1])
+        rows = slice(k * SUB, (k + 1) * SUB)
+        normed[rows, :] = inputs[rows, :].astype(F32) * inv_rms[rows, 0:1]
+        hid[k, y, z] = (normed[rows, :] * gain[...]).astype(BF16)
+        if k == 0:
+            hid1.append(gather1(hid, 0))
+    mask_weights(wd, ed, loads[0])
     arrive(hid1[0])
     hid2 = [gather2(hid, 0)]
     for k in (1, 2):
         cot1.append(gather1(cot, k))
         hid1.append(gather1(hid, k))
+    widen(mask_gate[...], eg)
     widen(mask_up[...], eu)
-    mask_weights(wu, eu, loads[2])
+    mask_weights(wg, eg, loads[1])
 
     def chunk_of(ref, k):
         return ref[k].reshape(4 * 4 * SUB, FEATS)
@@ -404,7 +405,15 @@
         for half, lanes in enumerate(halves):
             d_norm[rows, lanes] = row_total(1, k, half)
 
-    def weight_grad(left_of, right, wide_mask, target, stage, sems, first, last, reuse):
+    def early_grad(left_of, right, early, first, last):
+        def body(m, carry):
+            at = pl.multiple_of(m * TILE, TILE)
+            early[m] = tn_dot(left_of(0, 2, at), right(0, 2)).astype(BF16)
+            return carry
+
+        lax.fori_loop(first, last, body, 0)
+
+    def weight_grad(left_of, right, early, wide_mask, target, stage, sems, first, last, reuse):
         def body(m, carry):
             at = pl.multiple_of(m * TILE, TILE)
             use = lax.rem(m, 2)
@@ -419,26 +428,44 @@
                 def _():
                     store().wait()
 
-            stage[use] = masked(tn_dot(left_of(at), right()), wide_mask[pl.ds(m * 4, 4)])
+            product = tn_dot(left_of(2, 3, at), right(2, 3)) + early[m].astype(F32)
+            stage[use] = masked(product, wide_mask[pl.ds(m * 4, 4)])
             store().start()
             return carry
 
         lax.fori_loop(first, last, body, 0)
 
-    tokens = CHUNKS * 256
+    def act_of(start, width):
+        def get(k0, k1):
+            return act[k0:k1, :, start : start + width].reshape((k1 - k0) * 256, width)
+
+        return get
+
+    def act_left(k0, k1, at):
+        return act[k0:k1, :, pl.ds(at, TILE)].reshape((k1 - k0) * 256, TILE)
+
+    def cot_right(k0, k1):
+        return cot[k0:k1].reshape((k1 - k0) * 256, FEATS)
+
+    def hid_left(k0, k1, at):
+        return hid[k0:k1, :, :, :, pl.ds(at, TILE)].reshape((k1 - k0) * 256, TILE)
+
+    d_gate_right = act_of(UNITS, UNITS)
+
+    def early_down(first, last):
+        early_grad(act_left, cot_right, down_early, first, last)
+
+    def early_gate(first, last):
+        early_grad(hid_left, d_gate_right, gate_early, first, last)
 
     def grad_down(first, last, reuse):
         weight_grad(
-            lambda at: act[:, :, pl.ds(at, TILE)].reshape(tokens, TILE),
-            lambda: cot[...].reshape(tokens, FEATS),
-            ed, grad_w_down, stage_d, store_sem.at[0], first, last, reuse,
+            act_left, cot_right, down_early, ed, grad_w_down, stage_d, store_sem.at[0], first, last, reuse
         )
 
     def grad_gate(first, last, reuse):
         weight_grad(
-            lambda at: hid[:, :, :, :, pl.ds(at, TILE)].reshape(tokens, TILE),
-            lambda: act[:, :, UNITS : 2 * UNITS].reshape(tokens, UNITS),
-            eg, grad_w_gate, stage_u, store_sem.at[1], first, last, reuse,
+            hid_left, d_gate_right, gate_early, eg, grad_w_gate, stage_u, store_sem.at[1], first, last, reuse
         )
 
     all_job, out_job, in_job = (0, 3 * UNITS), (0, UNITS), (UNITS, 2 * UNITS)
@@ -447,6 +474,7 @@
     cot2.append(gather2(cot, 1))
     sd0 = scatter1(0, down_job, pd0)
     pg0 = mm_gate(0)
+    mask_weights(wu, eu, loads[2])
     pu0 = mm_up(0)
     arrive(hid1[1])
     hid2.append(gather2(hid, 1))
@@ -488,24 +516,27 @@
     r1 = spread3(1, all_job, h1, q1)
     n0 = row_scatters2(1, 0, n0)
     o0 = row_scatters2(0, 0, o0)
+    n1 = mm_in_back(1, r1)
     h2, q2 = spread2(2, in_job, a2)
+    o1 = mm_out(1, ())
+    early_gate(0, 2)
     u2, v2 = spread2(2, out_job, b2)
-    n1 = mm_in_back(1, r1)
-    o1 = mm_out(1, ())
+    early_gate(2, 4)
+    r2 = spread3(2, in_job, h2, q2)
+    n1 = row_scatters2(1, 1, n1)
+    w2 = spread3(2, out_job, u2, v2)
+    early_down(0, 3)
+    n2 = mm_in_back(2, r2)
+    o2 = mm_out(2, w2)
+    o1 = row_scatters2(0, 1, o1)
     finish_out(0, o0)
     finish_in(0, n0)
-    r2 = spread3(2, in_job, h2, q2)
-    n1 = row_scatters2(1, 1, n1)
-    o1 = row_scatters2(0, 1, o1)
-    n2 = mm_in_back(2, r2)
-    w2 = spread3(2, out_job, u2, v2)
-    finish_out(1, o1)
     finish_in(1, n1)
-    grad_gate(0, 1, False)
-    o2 = mm_out(2, w2)
+    early_down(3, 7)
     n2 = row_scatters2(1, 2, n2)
-    grad_gate(1, 2, False)
+    grad_gate(0, 2, False)
     o2 = row_scatters2(0, 2, o2)
+    grad_gate(2, 4, True)
     finish_in(2, n2)
 
     moved = d_norm[...] * normed[...]
@@ -513,9 +544,9 @@
     inner = all_col(in_own, in_in)
     gn_own[...] = jnp.sum(moved, axis=0, keepdims=True)
     gains = [send(gn_own, gn_in.at[index], device) for index, device in enumerate(row_peers)]
-    grad_gate(2, 4, True)
+    finish_out(1, o1)
+    grad_down(0, 4, False)
     finish_out(2, o2)
-    grad_down(0, 1, False)
     arrive(inner)
     inner_all = in_own[...]
     for index in range(7):
@@ -530,7 +561,7 @@
     for index in range(15):
         gain_total = gain_total + gn_in[index]
     grad_gain[...] = gain_total
-    grad_down(1, 7, False)
+    grad_down(4, 7, True)
     for use in range(2):
         pltpu.make_async_copy(stage_d.at[use], grad_w_down.at[pl.ds(0, TILE), :], store_sem.at[0, use]).wait()
         pltpu.make_async_copy(stage_u.at[use], grad_w_gate.at[pl.ds(0, TILE), :], store_sem.at[1, use]).wait()
@@ -559,10 +590,11 @@
     for source, held, target in ((grad_w_gate_in, big_a, grad_w_gate), (grad_w_down_in, big_b, grad_w_down)):
         rows = source.shape[0] // 4
         moves += [(source, held, target, slice(n * rows, (n + 1) * rows)) for n in range(4)]
-    loads, saves = [], []
-    for index, (source, held, target, rows) in enumerate(moves):
-        loads.append(pltpu.make_async_copy(source.at[rows, :], held.at[rows, :], in_sem.at[index]))
-        loads[-1].start()
+    loads = [
+        pltpu.make_async_copy(source.at[rows, :], held.at[rows, :], in_sem.at[index])
+        for index, (source, held, target, rows) in enumerate(moves)
+    ]
+    saves = []
 
     def move(count):
         for _ in range(count):
@@ -575,6 +607,8 @@
     widen(mask_up[...], eu)
     for need in needs:
         need.wait()
+    for load in loads:
+        load.start()
     grads = []
     tokens = CHUNKS * 256
     for m in range(FEATS // TILE):
@@ -609,6 +643,8 @@
         in_specs=[vmem, vmem, anywhere, anywhere, anywhere, vmem, vmem, vmem, vmem],
         out_specs=(vmem, vmem, vmem, anywhere, anywhere, anywhere, anywhere),
         scratch_shapes=[
+            pltpu.VMEM((FEATS // TILE, TILE, UNITS), BF16),
+            pltpu.VMEM((UNITS // TILE, TILE, FEATS), BF16),
             pltpu.VMEM((FEATS, UNITS), BF16),
             pltpu.VMEM((FEATS, UNITS), BF16),
             pltpu.VMEM((UNITS, FEATS), BF16),

time: 142 us -> 134 us (0.944)
  Pallas kernels: 141 us -> 133 us
    pallas_call x1, Pallas kernels: 130 us -> 124 us  [shards(): pl.pallas_call(layer, out_shape=(shape((LOCAL, FEATS), BF16), shape((LOCA...]
    pallas_call x1, Pallas kernels: 11.2 us -> 9.24 us  [shards(): pl.pallas_call(last_grad, out_shape=(shape((LOCAL, FEATS), BF16), shape((...]
where the time goes in v3:
time: 134 us
  Pallas kernels  133 us (99%)
    pallas_call x1, Pallas kernels, shards(): pl.pallas_call(layer, out_shape=(shape((LOCAL, FEATS), BF16), shape((LOCA...  124 us
    pallas_call x1, Pallas kernels, shards(): pl.pallas_call(last_grad, out_shape=(shape((LOCAL, FEATS), BF16), shape((...  9.24 us

profile of v3, /device:TPU:1, one launch (start us, length us, event | category | flops | bytes accessed | tf_op | source)
XLA Modules:
  0.0 133.7 jit_solution(7407429636401094592)
XLA Ops:
  0.6 123.7 %layer.1 = (bf16[48,1024]{1,0:T(8,128)(2,1)}, bf16[48,1024]{1,0:T(8,128)(2,1)}, f32[1,1024]{1,0:T(1,128)}, bf16[1024,1792]{1,0:T(8,128)(2,1)}, bf16[1792,1024]{1...) custom-call(bf16[48,1024]{1,0:T(8,128)(2,1)} %inputs.1, f32[1,1024]{1,0:T(1,128)} %bitcast.4, ...), custom_call_target="tpu_custom_call" | custom-call | tf_op jit(solution)/shard_map/layer/pallas_call | solution.py:632
  124.3 9.2 %last_grad.1 = (bf16[48,1024]{1,0:T(8,128)(2,1)}, bf16[48,1024]{1,0:T(8,128)(2,1)}, f32[1,1024]{1,0:T(1,128)}, bf16[1024,1792]{1,0:T(8,128)(2,1)}, bf16[1024,179...) custom-call(bf16[48,1024]{1,0:T(8,128)(2,1)} %get-tuple-element.19.output_in, ...), custom_call_target="tpu_custom_call" | custom-call | tf_op jit(solution)/shard_map/last_grad/pallas_call | solution.py:692

commit v4 on v3

--- a/solution.py
+++ b/solution.py
@@ -61,12 +61,13 @@
 
 
 def layer(
-    inputs, gain, w_gate, w_up, w_down, mask_gate, mask_up, mask_down, grad_out,
-    output, grad_inputs, grad_gain, grad_w_gate, grad_w_down, d_up_all, hid_all,
+    inputs_at, gain_at, w_gate, w_up, w_down, mask_gate_at, mask_up_at, mask_down_at, grad_out_at,
+    output_at, grad_inputs_at, grad_gain_at, grad_w_gate, grad_w_down, d_up_all, hid_all,
+    inputs, gain, mask_gate, mask_up, mask_down, grad_out, output, grad_inputs, grad_gain,
     gate_early, down_early, wg, wu, wd, eg, eu, ed, hid, cot, part, pair, fwd_a, fwd_b, from_l, from_r, act,
     row_part, row_in1, row_sum, row_in2, normed, inv_rms, d_norm,
     sq_own, sq_in, in_own, in_in, gn_own, gn_in, stage_d, stage_u,
-    send_sem, recv_sem, load_sem, store_sem, keep_sem,
+    send_sem, recv_sem, load_sem, store_sem, keep_sem, small_sem,
 ):
     row = lax.axis_index("row")
     col = lax.axis_index("col")
@@ -109,12 +110,15 @@
         for copy in copies:
             copy.wait_recv()
 
-    loads = [
-        pltpu.make_async_copy(source, target, load_sem.at[index])
-        for index, (source, target) in enumerate(((w_down, wd), (w_gate, wg), (w_up, wu)))
+    smalls = [
+        pltpu.make_async_copy(source, target, small_sem.at[index])
+        for index, (source, target) in enumerate((
+            (grad_out_at, grad_out), (inputs_at, inputs), (gain_at, gain),
+            (mask_down_at, mask_down), (mask_gate_at, mask_gate), (mask_up_at, mask_up),
+        ))
     ]
-    for load in loads:
-        load.start()
+    for small in smalls:
+        small.start()
 
     barrier = pltpu.get_barrier_semaphore()
     row_peers = [
@@ -126,6 +130,14 @@
     for device in neighbours:
         pl.semaphore_signal(barrier, inc=1, device_id=device, device_id_type=MESH)
 
+    loads = [
+        pltpu.make_async_copy(source, target, load_sem.at[index])
+        for index, (source, target) in enumerate(((w_down, wd), (w_gate, wg), (w_up, wu)))
+    ]
+    loads[0].start()
+
+    for small in smalls:
+        small.wait()
     for k in range(CHUNKS):
         cot[k, y, z] = grad_out[k * SUB : (k + 1) * SUB, :]
     wide = inputs[...].astype(F32)
@@ -174,6 +186,8 @@
         lax.fori_loop(0, wide_mask.shape[0], body, 0)
 
     widen(mask_down[...].astype(F32).T, ed)
+    widen(mask_gate[...], eg)
+    widen(mask_up[...], eu)
     arrive(cot1[0])
     cot2 = [gather2(cot, 0)]
 
@@ -191,15 +205,12 @@
         hid[k, y, z] = (normed[rows, :] * gain[...]).astype(BF16)
         if k == 0:
             hid1.append(gather1(hid, 0))
+            loads[1].start()
+            loads[2].start()
     mask_weights(wd, ed, loads[0])
     arrive(hid1[0])
     hid2 = [gather2(hid, 0)]
-    for k in (1, 2):
-        cot1.append(gather1(cot, k))
-        hid1.append(gather1(hid, k))
-    widen(mask_gate[...], eg)
-    widen(mask_up[...], eu)
-    mask_weights(wg, eg, loads[1])
+    cot1.append(gather1(cot, 1))
 
     def chunk_of(ref, k):
         return ref[k].reshape(4 * 4 * SUB, FEATS)
@@ -334,9 +345,9 @@
 
     halves = (slice(0, HALF), slice(HALF, FEATS))
 
-    def row_scatter1(which, k, half):
+    def row_scatter1(which, k, half, start=0, width=HALF):
         copies = []
-        lanes = pl.ds(half * HALF, HALF)
+        lanes = pl.ds(half * HALF + start, width)
         for steps in (1, 2, 3):
             into = row_in1.at[which, k, steps - 1, :, :, lanes]
             if half == 0:
@@ -366,7 +377,7 @@
         return after
 
     def row_scatters2(which, k, copies):
-        return row_scatter2(which, k, 0, copies[0:3]) + row_scatter2(which, k, 1, copies[3:6])
+        return row_scatter2(which, k, 0, copies[0]) + row_scatter2(which, k, 1, copies[1])
 
     def row_total(which, k, half):
         lanes = halves[half]
@@ -379,18 +390,21 @@
         arrive(pairs)
         product = nn_dot(act[k, :, 0:UNITS], wd[...]).astype(BF16)
         row_part[0, k] = product.reshape(4, 4, SUB, FEATS)
-        return row_scatter1(0, k, 0) + row_scatter1(0, k, 1)
-
-    def mm_in_back(k, pairs):
+        return row_scatter1(0, k, 0), row_scatter1(0, k, 1)
+
+    def mm_in_back(k, pairs, pieces=1):
         arrive(pairs)
         keep(act.at[k, :, pl.ds(2 * UNITS, UNITS)], d_up_all.at[k])
-        copies = []
-        for half, lanes in enumerate(halves):
-            product = nt_dot(act[k, :, UNITS : 2 * UNITS], wg[lanes, :]) + nt_dot(
-                act[k, :, 2 * UNITS : 3 * UNITS], wu[lanes, :]
-            )
-            row_part[1, k, :, :, :, lanes] = product.astype(BF16).reshape(4, 4, SUB, HALF)
-            copies += row_scatter1(1, k, half)
+        copies = ([], [])
+        width = HALF // pieces
+        for piece in range(pieces):
+            for half in range(2):
+                lanes = slice(half * HALF + piece * width, half * HALF + (piece + 1) * width)
+                product = nt_dot(act[k, :, UNITS : 2 * UNITS], wg[lanes, :]) + nt_dot(
+                    act[k, :, 2 * UNITS : 3 * UNITS], wu[lanes, :]
+                )
+                row_part[1, k, :, :, :, lanes] = product.astype(BF16).reshape(4, 4, SUB, width)
+                copies[half].extend(row_scatter1(1, k, half, piece * width, width))
         return copies
 
     def finish_out(k, copies):
@@ -470,11 +484,15 @@
 
     all_job, out_job, in_job = (0, 3 * UNITS), (0, UNITS), (UNITS, 2 * UNITS)
     pd0 = mm_down_back(0)
+    hid1.append(gather1(hid, 1))
     arrive(cot1[1])
     cot2.append(gather2(cot, 1))
+    mask_weights(wg, eg, loads[1])
     sd0 = scatter1(0, down_job, pd0)
+    cot1.append(gather1(cot, 2))
+    hid1.append(gather1(hid, 2))
+    mask_weights(wu, eu, loads[2])
     pg0 = mm_gate(0)
-    mask_weights(wu, eu, loads[2])
     pu0 = mm_up(0)
     arrive(hid1[1])
     hid2.append(gather2(hid, 1))
@@ -507,12 +525,12 @@
     td2 = scatter2(2, down_job, sd2)
     r0 = spread3(0, all_job, h0, q0)
     tg2 = scatter2(2, gate_up_job, sg2)
+    n0 = mm_in_back(0, r0)
     h1, q1 = spread2(1, all_job, a1)
-    n0 = mm_in_back(0, r0)
-    o0 = mm_out(0, ())
     activate(2, td2 + tg2)
     a2 = spread1(2, in_job)
     b2 = spread1(2, out_job)
+    o0 = mm_out(0, ())
     r1 = spread3(1, all_job, h1, q1)
     n0 = row_scatters2(1, 0, n0)
     o0 = row_scatters2(0, 0, o0)
@@ -526,7 +544,7 @@
     n1 = row_scatters2(1, 1, n1)
     w2 = spread3(2, out_job, u2, v2)
     early_down(0, 3)
-    n2 = mm_in_back(2, r2)
+    n2 = mm_in_back(2, r2, 2)
     o2 = mm_out(2, w2)
     o1 = row_scatters2(0, 1, o1)
     finish_out(0, o0)
@@ -537,6 +555,8 @@
     grad_gate(0, 2, False)
     o2 = row_scatters2(0, 2, o2)
     grad_gate(2, 4, True)
+    finish_out(1, o1)
+    grad_down(0, 2, False)
     finish_in(2, n2)
 
     moved = d_norm[...] * normed[...]
@@ -544,9 +564,9 @@
     inner = all_col(in_own, in_in)
     gn_own[...] = jnp.sum(moved, axis=0, keepdims=True)
     gains = [send(gn_own, gn_in.at[index], device) for index, device in enumerate(row_peers)]
-    finish_out(1, o1)
-    grad_down(0, 4, False)
     finish_out(2, o2)
+    keep(output, output_at)
+    grad_down(2, 7, True)
     arrive(inner)
     inner_all = in_own[...]
     for index in range(7):
@@ -556,12 +576,13 @@
         grad_out[...].astype(F32)
         + inv_rms[:, 0:1] * (d_norm[...] * gain[...] - normed[...] * row_inner)
     ).astype(BF16)
+    keep(grad_inputs, grad_inputs_at)
     arrive(gains)
     gain_total = gn_own[...]
     for index in range(15):
         gain_total = gain_total + gn_in[index]
     grad_gain[...] = gain_total
-    grad_down(4, 7, True)
+    keep(grad_gain, grad_gain_at)
     for use in range(2):
         pltpu.make_async_copy(stage_d.at[use], grad_w_down.at[pl.ds(0, TILE), :], store_sem.at[0, use]).wait()
         pltpu.make_async_copy(stage_u.at[use], grad_w_gate.at[pl.ds(0, TILE), :], store_sem.at[1, use]).wait()
@@ -640,9 +661,18 @@
             shape((CHUNKS, 256, UNITS), BF16),
             shape((CHUNKS, 4, 4, SUB, FEATS), BF16),
         ),
-        in_specs=[vmem, vmem, anywhere, anywhere, anywhere, vmem, vmem, vmem, vmem],
-        out_specs=(vmem, vmem, vmem, anywhere, anywhere, anywhere, anywhere),
+        in_specs=[anywhere] * 9,
+        out_specs=(anywhere,) * 7,
         scratch_shapes=[
+            pltpu.VMEM((LOCAL, FEATS), BF16),
+            pltpu.VMEM((1, FEATS), F32),
+            pltpu.VMEM((FEATS // BLOCK, UNITS // BLOCK), jnp.int32),
+            pltpu.VMEM((FEATS // BLOCK, UNITS // BLOCK), jnp.int32),
+            pltpu.VMEM((FEATS // BLOCK, UNITS // BLOCK), jnp.int32),
+            pltpu.VMEM((LOCAL, FEATS), BF16),
+            pltpu.VMEM((LOCAL, FEATS), BF16),
+            pltpu.VMEM((LOCAL, FEATS), BF16),
+            pltpu.VMEM((1, FEATS), F32),
             pltpu.VMEM((FEATS // TILE, TILE, UNITS), BF16),
             pltpu.VMEM((UNITS // TILE, TILE, FEATS), BF16),
             pltpu.VMEM((FEATS, UNITS), BF16),
@@ -679,7 +709,8 @@
             pltpu.SemaphoreType.DMA((COPIES,)),
             pltpu.SemaphoreType.DMA((3,)),
             pltpu.SemaphoreType.DMA((2, 2)),
-            pltpu.SemaphoreType.DMA((2 * CHUNKS,)),
+            pltpu.SemaphoreType.DMA((2 * CHUNKS + 3,)),
+            pltpu.SemaphoreType.DMA((6,)),
         ],
         compiler_params=pltpu.CompilerParams(
             collective_id=0, has_side_effects=True, vmem_limit_bytes=60 << 20

time: 134 us -> 131 us (0.978)
  Pallas kernels: 133 us -> 130 us
    pallas_call x1, Pallas kernels: 124 us -> 121 us  [shards(): pl.pallas_call(layer, out_shape=(shape((LOCAL, FEATS), BF16), shape((LOCA...]
where the time goes in v4:
time: 131 us
  Pallas kernels  130 us (99%)
    pallas_call x1, Pallas kernels, shards(): pl.pallas_call(layer, out_shape=(shape((LOCAL, FEATS), BF16), shape((LOCA...  121 us
    pallas_call x1, Pallas kernels, shards(): pl.pallas_call(last_grad, out_shape=(shape((LOCAL, FEATS), BF16), shape((...  9.24 us

profile of v4, /device:TPU:1, one launch (start us, length us, event | category | flops | bytes accessed | tf_op | source)
XLA Modules:
  0.0 131.3 jit_solution(5886732031054018868)
XLA Ops:
  0.6 121.2 %layer.1 = (bf16[48,1024]{1,0:T(8,128)(2,1)}, bf16[48,1024]{1,0:T(8,128)(2,1)}, f32[1,1024]{1,0:T(1,128)}, bf16[1024,1792]{1,0:T(8,128)(2,1)}, bf16[1792,1024]{1...) custom-call(bf16[48,1024]{1,0:T(8,128)(2,1)} %inputs_at.1, f32[1,1024]{1,0:T(1,128)} %bitcast.4, ...), custom_call_target="tpu_custom_call" | custom-call | tf_op jit(solution)/shard_map/layer/pallas_call | solution.py:653
  121.9 9.2 %last_grad.1 = (bf16[48,1024]{1,0:T(8,128)(2,1)}, bf16[48,1024]{1,0:T(8,128)(2,1)}, f32[1,1024]{1,0:T(1,128)}, bf16[1024,1792]{1,0:T(8,128)(2,1)}, bf16[1024,179...) custom-call(bf16[48,1024]{1,0:T(8,128)(2,1)} %get-tuple-element.19.output_in, ...), custom_call_target="tpu_custom_call" | custom-call | tf_op jit(solution)/shard_map/last_grad/pallas_call | solution.py:723
